TPU v7x, 128 devices: a whole 4x4x4 slice. The times are simulated.
128 devices in a mesh: grp: 4 (over y), seq: 32 (over z, x, core).
Axes of the slice: x: 4, y: 4, z: 4, core: 2. Of those that a mesh axis runs over, the one named last changes fastest.
Arguments:
- hidden_in: bfloat16 [114688, 1024], P(('grp', 'seq')), may hold values from -16 to 16
- attn_gain: float32 [1024], replicated, may hold values from 0.1 to 1.9
- w_qkv: bfloat16 [1024, 3072], replicated
- head_gain: float32 [1024], replicated, may hold values from 0.1 to 1.9
- w_out: bfloat16 [1024, 1024], replicated, may hold values from -0.1875 to 0.1875
- ffn_gain: float32 [1024], replicated, may hold values from 0.1 to 1.9
- w_gate: bfloat16 [32, 1024, 896], P('seq'), may hold values from -0.1875 to 0.1875
- w_up: bfloat16 [32, 1024, 896], P('seq'), may hold values from -0.1875 to 0.1875
- w_down: bfloat16 [32, 896, 1024], P('seq'), may hold values from -0.1875 to 0.1875
- pair_ids: int32 [896, 2], P(('grp', 'seq')), may hold values from 0 to 31, as said below
- gate_codes: int32 [896, 2], P(('grp', 'seq')), may hold values from 1 to 255
Outputs:
- layer_out: bfloat16 [114688, 1024], P(('grp', 'seq'))
Inputs may be any that keep to these rules, and one draw needn't show every extreme that they name: `pair_ids`: each row names two different experts. Within the 7 rows of one device (aligned blocks of 7 rows) no expert is named more than 2 times, and some expert exactly 2 times. Within the rows of one group (aligned blocks of 224 rows) exactly one expert is named 28 times, every other at most 14 times and some other exactly 14 times; the expert named 28 times differs from group to group.
All inputs are finite; a program needn't handle non-finite values.
Results may differ from a plain program's by a relative error of at most 0.0055.
Values may be sent and summed in bfloat16 or wider, within the bound.
A program may use at most 192 MiB of HBM per device.

v0:
```python
import functools

import jax
import jax.numpy as jnp
from jax import lax
from jax.experimental import pallas as pl
from jax.experimental.pallas import tpu as pltpu
from jax.sharding import PartitionSpec as P

HEADS = 8
HEAD_DIM = 128
ROWS = 128
EPS = 1e-06
WAYS = 4
CORES = 2
SLOTS = 2
SIDES = 2
PART = SIDES * SLOTS
CHUNKS = 8
STATE = 144
LIMIT = 8
LANES = 128
HALF = 512
SLICE = 64
PIECE = 16
HOT = 15
MESH = pl.DeviceIdType.MESH
F32 = jnp.float32
BF16 = jnp.bfloat16
LIMIT_BYTES = 60 * 1024 * 1024


def place():
    seq = lax.axis_index("seq")
    return lax.axis_index("grp"), seq // (WAYS * CORES), (seq // CORES) % WAYS, seq % CORES


def remote(src, dst, send, recv, device):
    return pltpu.make_async_remote_copy(
        src_ref=src, dst_ref=dst, send_sem=send, recv_sem=recv, device_id=device, device_id_type=MESH
    )


def greet(devices):
    barrier = pltpu.get_barrier_semaphore()
    for device in devices:
        pl.semaphore_signal(barrier, inc=1, device_id=device, device_id_type=MESH)
    pl.semaphore_wait(barrier, len(devices))


def norm_rows(values, gain):
    return values * lax.rsqrt(jnp.mean(values * values, axis=-1, keepdims=True) + EPS) * gain


def dot_last(a, b):
    return lax.dot_general(a, b, (((1,), (1,)), ((), ())), preferred_element_type=F32)


def dot_first(a, b):
    return lax.dot_general(a, b, (((0,), (0,)), ((), ())), preferred_element_type=F32)


def lifted(values):
    return jnp.where(values > 0.0, values + 1.0, jnp.exp(jnp.minimum(values, 0.0))).astype(BF16)


def tables(turn, ids, rank, shares, hot, out_int, out_real):
    y, z, x, c = place()
    half = x // 2
    other = (x + 2 * (x % 2) - 1 + WAYS) % WAYS
    span = LANES * 7 // 16
    lane = lax.broadcasted_iota(jnp.int32, (1, LANES), 1)
    local = lane - half * span
    near = (local >= 0) & (local < span)
    place_of = rank - turn * SLOTS
    usable = near & (ids >= 0) & (ids != hot) & (place_of >= 0) & (place_of < SLOTS)
    slot = lax.broadcasted_iota(jnp.int32, (16, LANES), 0)
    column = jnp.where(slot >= 8, other, x)
    expert = ((slot & 7) >> 1) * (WAYS * CORES) + column * CORES + c
    key = jnp.where(usable, ids * SLOTS + place_of, -1)
    hit = key == expert * SLOTS + (slot & 1)
    source = jnp.sum(jnp.where(hit, local >> 1, 0).astype(F32), axis=1, keepdims=True)
    out_int[0:16, :] = jnp.broadcast_to(source, (16, LANES)).astype(jnp.int32)
    here = (ids >> 1) & 3
    which = jnp.where(here == other, 1, 0)
    mine = usable & ((here == x) | (here == other))
    index = (ids & 1) * 16 + which * 8 + (ids >> 3) * SLOTS + place_of
    out_int[16:17, :] = jnp.where(mine, index, 0)
    out_real[0:1, :] = jnp.where(mine, shares, 0.0)


def front_kernel(
    groups, blocks, pairs, codes, x_ref, again_ref, wqkv_ref, hgain_ref, wout_ref, fgain_ref,
    wg_ref, wu_ref, wd_ref, resid_ref, ffn_ref, int_ref, real_ref, hot_ref,
    normed, q, k, v, wcols, state, ratio, numer, denom,
    chip, chips, sib, rows, peak, peaks,
    mine, theirs, sums, xs, row_sum, zs, plane_sum, ys, back, heads_in, sib2,
    near, far, slices, halves_in, summed, pieces_in, loads, stay, send, recv,
):
    y, z, x, c = place()
    lane_count = WAYS * CORES
    tokens, width = x_ref.shape
    tiles = tokens // ROWS
    step = 2 * HEAD_DIM
    steps = width // step

    def at(yy, zz, xx, cc):
        return (yy, zz * lane_count + xx * CORES + cc)

    sibling = at(y, z, x, 1 - c)
    along_x = [at(y, z, (x + d) % WAYS, c) for d in range(1, WAYS)]
    along_z = [at(y, (z + d) % WAYS, x, c) for d in range(1, WAYS)]
    along_y = [at((y + d) % groups, z, x, c) for d in range(1, groups)]
    fetches = []
    for j in range(3 * steps):
        fetch = pltpu.make_async_copy(
            wqkv_ref.at[:, pl.ds(j * step, step)], wcols.at[j], loads.at[j]
        )
        fetch.start()
        fetches.append(fetch)
    greet([sibling] + along_x + along_z + along_y)
    copies = []

    def go(src, dst, device):
        n = len(copies)
        copy = remote(src, dst, send.at[n], recv.at[n], device)
        copy.start()
        copies.append(copy)
        return copy

    def arrive(waits):
        for copy in waits:
            copy.wait_recv()

    hidden = wg_ref.shape[1]
    offset = wd_ref.shape[0] - HALF
    lanes_of = (
        (wg_ref, HALF, pl.ds(0, hidden)),
        (wu_ref, HALF, pl.ds(hidden, hidden)),
        (wd_ref, offset, pl.ds(2 * hidden, width)),
    )
    ring = (
        (x, along_x[0], along_x[2], along_x[1]),
        (z, along_z[0], along_z[2], along_z[1]),
    )
    swapped = []
    for n, (source, jump, span) in enumerate(lanes_of):
        there = source.at[pl.ds(jump * (1 - c), HALF), :]
        swapped.append(go(there, far.at[:, span], sibling))
        local = pltpu.make_async_copy(
            source.at[pl.ds(jump * c, HALF), :], near.at[:, span], stay.at[n]
        )
        local.start()
        fetches.append(local)

    def start_reduce(far_half):
        waits = []
        for order, (spot, plus, minus, _) in enumerate(ring):
            top = order * (HALF // 2)

            def part(i, shift=0, size=SLICE):
                row = top + ((spot + i + WAYS) % WAYS) * SLICE + shift
                return near.at[pl.ds(row, size)]

            short = SLICE // 2
            if far_half:
                waits.append(
                    (
                        go(part(2, 0, short), halves_in.at[order, 0], plus),
                        go(part(2, short, short), halves_in.at[order, 1], minus),
                    )
                )
            else:
                waits.append(
                    (
                        go(part(1), slices.at[order, 0], plus),
                        go(part(-1), slices.at[order, 1], minus),
                    )
                )
        return waits

    def relay_reduce(waits):
        short = SLICE // 2
        for order, (_, plus, minus, _) in enumerate(ring):
            arrive(waits[order])
            waits[order] = (
                go(halves_in.at[order, 0], slices.at[order, 2, pl.ds(0, short)], plus),
                go(halves_in.at[order, 1], slices.at[order, 2, pl.ds(short, short)], minus),
            )

    def second_reduce(waits):
        later = []
        for order, (spot, _, _, _) in enumerate(ring):
            arrive(waits[order])
            top = order * (HALF // 2) + spot * SLICE

            @pl.loop(0, SLICE // PIECE)
            def _(i):
                row = pl.multiple_of(i * PIECE, PIECE)
                base_rows = pl.ds(pl.multiple_of(top + row, PIECE), PIECE)
                row = pl.ds(row, PIECE)
                total = near[base_rows, :] + slices[order, 0, row, :]
                summed[order, row, :] = total + (slices[order, 1, row, :] + slices[order, 2, row, :])

            spot, plus, minus, opposite = ring[1 - order]
            for d, device in ((1, plus), (2, opposite), (3, minus)):
                piece = summed.at[order, pl.ds(((spot + d) % WAYS) * PIECE, PIECE)]
                later.append(go(piece, pieces_in.at[order, d - 1], device))
        return later

    def gather_pieces(waits):
        arrive(waits)
        later = []
        for order in range(2):
            spot, plus, minus, opposite = ring[1 - order]
            row = pl.ds(pl.multiple_of(spot * PIECE, PIECE), PIECE)
            total = summed[order, row, :] + pieces_in[order, 0]
            hot_ref[order, row, :] = total + (pieces_in[order, 1] + pieces_in[order, 2])
            for device in (plus, opposite, minus):
                later.append(go(hot_ref.at[order, row], hot_ref.at[order, row], device))
        return later

    visits = 2 * blocks
    lane = lax.broadcasted_iota(jnp.int32, (8, LANES), 1)
    sub = lax.broadcasted_iota(jnp.int32, (8, LANES), 0)
    first = (x * CORES + c) * visits
    info = jnp.zeros((8, LANES), jnp.int32)
    for b in range(blocks):
        both = codes[b, 0] + codes[b, 1]
        for j in range(2):
            here = lane == first + (2 * b + j)
            value = jnp.where(sub == 0, pairs[b, j] + 1, jnp.where(sub == 1, codes[b, j], both))
            info = jnp.where(here & (sub < 3), value, info)
    chip[...] = info
    waits = [go(chip, sib, sibling)]

    @pl.loop(0, tiles)
    def _(i):
        rows_i = pl.ds(pl.multiple_of(i * ROWS, ROWS), ROWS)
        normed[rows_i, :] = norm_rows(x_ref[rows_i, :].astype(F32), again_ref[...]).astype(BF16)

    arrive(waits)
    chips[x] = info + sib[...]
    waits = [go(chips.at[x], chips.at[x], device) for device in along_x]

    def project(j):
        for part in range(3):
            fetches[part * steps + j].wait()
        cols = slice(j * step, (j + 1) * step)
        q[:, cols] = lifted(jnp.dot(normed[...], wcols[j], preferred_element_type=F32))
        k[:, cols] = lifted(jnp.dot(normed[...], wcols[steps + j], preferred_element_type=F32))
        v[:, cols] = jnp.dot(
            normed[...], wcols[2 * steps + j], preferred_element_type=F32
        ).astype(BF16)
        for head in range(2 * j, 2 * j + 2):
            cols = slice(head * HEAD_DIM, (head + 1) * HEAD_DIM)
            keys = k[:, cols]
            total = jnp.sum(keys.astype(F32), axis=0, keepdims=True)
            total = jnp.broadcast_to(total, (STATE - HEAD_DIM, HEAD_DIM))
            outer = dot_first(v[:, cols], keys)
            state[head, :HEAD_DIM, :] = outer
            state[head, HEAD_DIM:, :] = total
            mine[head, :HEAD_DIM, :] = outer.astype(BF16)
            mine[head, HEAD_DIM:, :] = total.astype(BF16)

    project(0)
    arrive(waits)
    info_row = chips[0] + chips[1] + chips[2] + chips[3]
    rows[z] = info_row
    waits = [go(rows.at[z], rows.at[z], device) for device in along_z]
    project(1)
    arrive(waits)
    expert = lax.broadcasted_iota(jnp.int32, (WAYS * lane_count, LANES), 0)
    lanes = lax.broadcasted_iota(jnp.int32, (WAYS * lane_count, LANES), 1)
    counts = jnp.zeros((WAYS * lane_count, 1), F32)
    most = jnp.zeros((WAYS * lane_count, 1), F32)
    for i in range(WAYS):
        there = (rows[i][0:1, :] - 1) == expert
        low = jnp.sum(jnp.where(there & (lanes < 4 * visits), 1.0, 0.0), axis=1, keepdims=True)
        high = jnp.sum(jnp.where(there & (lanes >= 4 * visits), 1.0, 0.0), axis=1, keepdims=True)
        counts = counts + low + high
        most = jnp.maximum(most, jnp.maximum(low, high))
    is_hot = counts > HOT - 0.5
    hot = jnp.sum(jnp.where(is_hot, expert[:, 0:1].astype(F32), 0.0), axis=0, keepdims=True)
    most = jnp.max(jnp.where(is_hot, 0.0, most), axis=0, keepdims=True)
    peak[...] = jnp.broadcast_to(most, (8, LANES))
    peak_waits = [go(peak, peaks.at[y], device) for device in along_y]
    here = (hot == (z * lane_count + x * CORES + c).astype(F32)).astype(BF16)
    beside = (hot == (z * lane_count + x * CORES + 1 - c).astype(F32)).astype(BF16)
    project(2)
    arrive(swapped)
    for fetch in fetches[-3:]:
        fetch.wait()

    @pl.loop(0, HALF // PIECE)
    def _(i):
        row = pl.ds(pl.multiple_of(i * PIECE, PIECE), PIECE)
        near[row, :] = near[row, :] * here + far[row, :] * beside

    reduce_waits = start_reduce(False)
    project(3)
    waits = [go(mine, theirs, sibling)]
    hot = jnp.broadcast_to(hot, (1, LANES)).astype(jnp.int32)
    ids = info_row[0:1, :] - 1
    wide = jnp.broadcast_to(ids, (LANES, LANES))
    tall = wide.T
    rank_lane = lax.broadcasted_iota(jnp.int32, (LANES, LANES), 1)
    rank_sub = lax.broadcasted_iota(jnp.int32, (LANES, LANES), 0)
    earlier = (wide == tall) & (rank_sub < rank_lane)
    halves = (rank_sub < 4 * visits) == (rank_lane < 4 * visits)
    rank = jnp.sum(jnp.where(earlier & halves, 1.0, 0.0), axis=0, keepdims=True).astype(jnp.int32)
    shares = info_row[1:2, :].astype(F32) / jnp.maximum(info_row[2:3, :], 1).astype(F32)
    int_ref[16:24, :] = jnp.zeros((8, LANES), jnp.int32)
    real_ref[...] = jnp.zeros((8, LANES), F32)
    tables(0, ids, rank, shares, hot, int_ref, real_ref)
    lane = lane[0:1, :]
    own = (lane >= first) & (lane < first + visits) & (ids == hot)
    seen = jnp.sum(jnp.where(own, 1.0, 0.0), axis=1, keepdims=True)
    first_lane = jnp.min(jnp.where(own, lane, 1000).astype(F32), axis=1, keepdims=True)
    last_lane = jnp.max(jnp.where(own, lane, -1).astype(F32), axis=1, keepdims=True)
    int_ref[17:18, :] = ids
    int_ref[18:19, :] = rank
    int_ref[19:20, :] = hot
    first_block = jnp.where(seen > 0.5, (first_lane.astype(jnp.int32) - first) >> 1, 0)
    last_block = (last_lane.astype(jnp.int32) - first) >> 1
    following = jnp.where(first_block + 1 >= blocks, 0, first_block + 1)
    second_block = jnp.where(seen > 1.5, last_block, following)
    int_ref[21:22, :] = jnp.where(lane == 0, first_block, second_block)
    lane_real = lane.astype(F32)
    first_share = jnp.sum(
        jnp.where(own & (lane_real == first_lane), shares, 0.0), axis=1, keepdims=True
    )
    last_share = jnp.sum(
        jnp.where(own & (lane_real == last_lane) & (seen > 1.5), shares, 0.0), axis=1, keepdims=True
    )
    real_ref[1:2, :] = shares
    real_ref[2:3, :] = jnp.where(lane == 0, first_share, last_share)
    arrive(peak_waits)
    peaks[y] = peak[...]
    top = peaks[0]
    for i in range(1, groups):
        top = jnp.maximum(top, peaks[i])
    int_ref[22:23, :] = top[0:1, :].astype(jnp.int32)

    causal = lax.broadcasted_iota(jnp.int32, (ROWS, ROWS), 0) >= lax.broadcasted_iota(
        jnp.int32, (ROWS, ROWS), 1
    )

    def within(start, stop):
        @pl.loop(start, stop)
        def _(head):
            cols = pl.ds(pl.multiple_of(head * HEAD_DIM, HEAD_DIM), HEAD_DIM)
            keys = k[:, cols]
            both = jnp.concatenate([v[:, cols], jnp.ones((tokens, HEAD_DIM), BF16)], axis=1)
            for tile in range(tiles):
                part = slice(tile * ROWS, (tile + 1) * ROWS)
                query = q[part, cols]
                scores = jnp.where(causal, dot_last(query, keys[part, :]), 0.0).astype(BF16)
                total = jnp.dot(scores, both[part, :], preferred_element_type=F32)
                if tile > 0:
                    scores = dot_last(query, keys[: tile * ROWS, :]).astype(BF16)
                    total = total + jnp.dot(
                        scores, both[: tile * ROWS, :], preferred_element_type=F32
                    )
                numer[part, cols] = total[:, :HEAD_DIM]
                denom[part, cols] = total[:, HEAD_DIM:]

    within(0, 2)
    arrive(waits)
    base = c * WAYS
    for i in range(WAYS):
        sums[i] = (state[base + i] + theirs[base + i].astype(F32)).astype(BF16)
    xs[x] = sums[x]
    waits = [go(sums.at[(x + d) % WAYS], xs.at[x], along_x[d - 1]) for d in range(1, WAYS)]
    far_waits = start_reduce(True)
    within(2, 4)
    arrive(waits)
    row_sum[...] = sum(xs[i].astype(F32) for i in range(WAYS)).astype(BF16)
    zs[z] = row_sum[...]
    waits = [go(row_sum, zs.at[z], along_z[d - 1]) for d in range(1, WAYS)]
    relay_reduce(far_waits)
    within(4, 6)
    arrive(waits)
    plane_sum[...] = sum(zs[i].astype(F32) for i in range(WAYS)).astype(BF16)
    waits = [go(plane_sum, ys.at[y], along_y[d - 1]) for d in range(1, groups)]
    total = jnp.zeros(row_sum.shape, F32)
    for i in range(WAYS):
        total = total + zs[i].astype(F32) * jnp.where(i < z, 1.0, 0.0)
    within(6, 7)
    arrive(waits)
    ys[y] = plane_sum[...]
    for i in range(groups):
        total = total + ys[i].astype(F32) * jnp.where(i < y, 1.0, 0.0)
    for i in range(WAYS):
        back[i] = total.astype(BF16)
        total = total + xs[i].astype(F32)
    heads_in[x] = back[x]
    waits = [go(back.at[(x + d) % WAYS], heads_in.at[x], along_x[d - 1]) for d in range(1, WAYS)]
    within(7, 8)
    reduce_waits = second_reduce([a + b for a, b in zip(reduce_waits, far_waits)])
    arrive(waits)
    waits = [go(heads_in, sib2, sibling)]
    later = jnp.where(c == 1, 1.0, 0.0)

    def add_prior(first_head, source):
        @pl.loop(0, WAYS)
        def _(i):
            head = first_head + i
            prior = (source[i].astype(F32) + theirs[head].astype(F32) * later).astype(BF16)
            filled = jnp.broadcast_to(prior[HEAD_DIM : HEAD_DIM + 1, :], (HEAD_DIM, HEAD_DIM))
            carried = jnp.concatenate([prior[:HEAD_DIM, :], filled], axis=0)
            cols = pl.ds(pl.multiple_of(head * HEAD_DIM, HEAD_DIM), HEAD_DIM)
            total = dot_last(q[:, cols], carried)
            ratio[:, cols] = (numer[:, cols] + total[:, :HEAD_DIM]) / (
                denom[:, cols] + total[:, HEAD_DIM:]
            )

    add_prior(base, heads_in)
    reduce_waits = gather_pieces(reduce_waits)
    arrive(waits)
    add_prior((1 - c) * WAYS, sib2)
    half = tokens // 2
    for part in range(2):
        part_rows = slice(part * half, (part + 1) * half)
        attended = norm_rows(ratio[part_rows, :], hgain_ref[...]).astype(BF16)
        resid = x_ref[part_rows, :].astype(F32) + jnp.dot(
            attended, wout_ref[...], preferred_element_type=F32
        )
        resid = resid.astype(BF16)
        resid_ref[part_rows, :] = resid
        ffn_ref[part_rows, :] = norm_rows(resid.astype(F32), fgain_ref[...]).astype(BF16)
    arrive(reduce_waits)
    for copy in copies:
        copy.wait_send()


def front(
    x, attn_gain, w_qkv, head_gain, w_out, ffn_gain, w_gate, w_up, w_down, pair_ids, gate_codes, groups
):
    tokens, width = x.shape
    packed = 2 * w_gate.shape[1] + width
    blocks = pair_ids.shape[0]
    tile = (8, LANES)
    one = (STATE, HEAD_DIM)
    some = (WAYS,) + one
    every = (HEADS,) + one
    step = 2 * HEAD_DIM
    pieces = 3 * width // step
    count = 1 + 2 * (WAYS - 1) + groups - 1 + 2 + 3 * (WAYS - 1) + groups - 1
    count += 3 + 12 + 4 * (WAYS - 1)

    def wide(*shape):
        return pltpu.VMEM(shape + (packed,), BF16)

    smem = pl.BlockSpec(memory_space=pltpu.SMEM)
    vmem = pl.BlockSpec(memory_space=pltpu.VMEM)
    hbm = pl.BlockSpec(memory_space=pl.ANY)
    return pl.pallas_call(
        functools.partial(front_kernel, groups, blocks),
        out_shape=[jax.ShapeDtypeStruct((tokens, width), BF16)] * 2
        + [jax.ShapeDtypeStruct((24, LANES), jnp.int32), jax.ShapeDtypeStruct(tile, F32)]
        + [jax.ShapeDtypeStruct((2, SLICE, packed), BF16)],
        in_specs=[smem] * 2 + [vmem] * 2 + [hbm] + [vmem] * 3 + [hbm] * 3,
        out_specs=[vmem] * 5,
        scratch_shapes=[pltpu.VMEM((tokens, width), BF16)] * 4
        + [pltpu.VMEM((pieces, width, step), BF16), pltpu.VMEM(every, F32)]
        + [pltpu.VMEM((tokens, width), F32)] * 3
        + [
            pltpu.VMEM(tile, jnp.int32),
            pltpu.VMEM((WAYS,) + tile, jnp.int32),
            pltpu.VMEM(tile, jnp.int32),
            pltpu.VMEM((WAYS,) + tile, jnp.int32),
            pltpu.VMEM(tile, F32),
            pltpu.VMEM((groups,) + tile, F32),
            pltpu.VMEM(every, BF16),
            pltpu.VMEM(every, BF16),
            pltpu.VMEM(some, BF16),
            pltpu.VMEM(some, BF16),
            pltpu.VMEM(one, BF16),
            pltpu.VMEM(some, BF16),
            pltpu.VMEM(one, BF16),
            pltpu.VMEM((groups,) + one, BF16),
            pltpu.VMEM(some, BF16),
            pltpu.VMEM(some, BF16),
            pltpu.VMEM(some, BF16),
            wide(HALF),
            wide(HALF),
            wide(2, WAYS - 1, SLICE),
            wide(2, 2, SLICE // 2),
            wide(2, SLICE),
            wide(2, WAYS - 1, PIECE),
            pltpu.SemaphoreType.DMA((pieces,)),
            pltpu.SemaphoreType.DMA((3,)),
            pltpu.SemaphoreType.DMA((count,)),
            pltpu.SemaphoreType.DMA((count,)),
        ],
        compiler_params=pltpu.CompilerParams(
            collective_id=0, has_side_effects=True, vmem_limit_bytes=LIMIT_BYTES
        ),
        name="front",
    )(
        pair_ids, gate_codes, x, attn_gain, w_qkv, head_gain, w_out, ffn_gain, w_gate, w_up, w_down
    )


def moe_kernel(
    blocks, chunks, table, weight, f_ref, base_ref, wg_ref, wu_ref, wd_ref, slice_ref, out_ref,
    *rest
):
    gather, landed = rest[:chunks], rest[chunks : 2 * chunks]
    (
        hand, zs, relay, taken, made_rows, relay_back, hand_back, partial, final, local, send, recv,
        hotw, hot_inner, hot_out, hot_local, hot_send, hot_recv,
    ) = rest[2 * chunks :]
    depth = ROWS // chunks
    width = f_ref.shape[2]
    y, z, x, c = place()
    lane = WAYS * CORES
    parity = x % 2

    def at(zz, xx, cc):
        return (y, ((zz + WAYS) % WAYS) * lane + ((xx + WAYS) % WAYS) * CORES + cc)

    sibling = at(z, x, 1 - c)
    mate = at(z, x + 1 - 2 * parity, c)
    across = at(z, x + 2 * parity - 1, c)
    up, down = at(z + 1, x, c), at(z - 1, x, c)
    greet([sibling, mate, across, up, down])
    me = parity * CORES + c
    friend = (1 - parity) * CORES + c
    pending = []
    made = {}

    def go(k, n, src, dst, device):
        copy = remote(src, dst, send.at[k, n], recv.at[k, n], device)
        copy.start()
        pending.append(copy)
        made[k, n] = copy

    def keep(k, n, src, dst):
        copy = pltpu.make_async_copy(src, dst, local.at[k, n])
        copy.start()
        made[k, "keep", n] = copy

    def arrived(k, *numbers):
        for n in numbers:
            made[k, n].wait_recv()

    def step_of(row):
        return (row + WAYS) % WAYS

    def begin(k):
        own = f_ref.at[:, pl.ds(k * depth, depth), :]
        here = gather[k].at[pl.ds(me * blocks, blocks)]
        go(k, 0, own, here, mate)
        go(k, 1, own, here, sibling)
        keep(k, 0, own, here)

    def widen(k):
        arrived(k, 0)
        there = gather[k].at[pl.ds(friend * blocks, blocks)]
        go(k, 2, there, there, sibling)

    def select(k):
        made[k, "keep", 0].wait()
        arrived(k, 1, 2)
        for row in range(WAYS):
            for j in range(SLOTS):
                hand[k, row, j] = gather[k][table[8 + row * SLOTS + j, 0]]
        go(k, 3, hand.at[k], zs.at[k, :, 1], across)
        for row in range(WAYS):
            for j in range(SLOTS):
                zs[k, row, 0, j] = gather[k][table[row * SLOTS + j, 0]]

    def climb(k):
        arrived(k, 3)
        go(k, 6, zs.at[k, step_of(z + 2), 0], relay.at[k, 0], up)
        go(k, 19, zs.at[k, step_of(z + 2), 1], relay.at[k, 1], down)
        go(k, 4, zs.at[k, step_of(z + 1)], taken.at[k, z], up)
        go(k, 5, zs.at[k, step_of(z - 1)], taken.at[k, z], down)
        keep(k, 1, zs.at[k, z], taken.at[k, z])

    def forward(k):
        arrived(k, 6)
        go(k, 7, relay.at[k, 0], taken.at[k, step_of(z - 1), 0], up)
        arrived(k, 19)
        go(k, 20, relay.at[k, 1], taken.at[k, step_of(z + 1), 1], down)

    def work(k):
        arrived(k, 4, 5, 7, 20)
        made[k, "keep", 1].wait()
        rows = taken[k].reshape(WAYS * PART * depth, width)
        gate = jnp.dot(rows, wg_ref[...], preferred_element_type=F32)
        upper = jnp.dot(rows, wu_ref[...], preferred_element_type=F32)
        inner = (jax.nn.silu(gate) * upper).astype(BF16)
        result = jnp.dot(inner, wd_ref[...], preferred_element_type=F32).astype(BF16)
        made_rows[k] = result.reshape(WAYS, SIDES, SLOTS, depth, width)
        go(k, 12, made_rows.at[k, step_of(z + 2), 0], relay_back.at[k, 0], up)
        go(k, 21, made_rows.at[k, step_of(z + 2), 1], relay_back.at[k, 1], down)
        for n, d, device in ((8, 1, up), (10, -1, down)):
            target = step_of(z + d)
            go(k, n, made_rows.at[k, target, 0], landed[k].at[pl.ds(c * 16 + z * SLOTS, SLOTS)], device)
            go(k, n + 1, made_rows.at[k, target, 1], hand_back.at[k, pl.ds(z * SLOTS, SLOTS)], device)
        keep(k, 2, made_rows.at[k, z, 0], landed[k].at[pl.ds(c * 16 + z * SLOTS, SLOTS)])
        keep(k, 3, made_rows.at[k, z, 1], hand_back.at[k, pl.ds(z * SLOTS, SLOTS)])

    def forward_back(k):
        arrived(k, 21)
        origin = step_of(z + 1)
        go(k, 14, relay_back.at[k, 1], hand_back.at[k, pl.ds(origin * SLOTS, SLOTS)], down)
        arrived(k, 12)
        origin = step_of(z - 1)
        go(k, 13, relay_back.at[k, 0], landed[k].at[pl.ds(c * 16 + origin * SLOTS, SLOTS)], up)

    def give(k):
        arrived(k, 9, 11, 14)
        made[k, "keep", 3].wait()
        go(k, 15, hand_back.at[k], landed[k].at[pl.ds(c * 16 + 8, 8)], across)
        arrived(k, 8, 10, 13)
        made[k, "keep", 2].wait()
        there = landed[k].at[pl.ds(c * 16, 8)]
        go(k, 16, there, there, sibling)

    def mirror(k):
        arrived(k, 15)
        there = landed[k].at[pl.ds(c * 16 + 8, 8)]
        go(k, 17, there, there, sibling)

    def build(k):
        arrived(k, 16, 17)

        def one(start, offset):
            def run(b, carry):
                first = start + 2 * b
                total = landed[k][table[16, first]].astype(F32) * weight[0, first]
                total = total + landed[k][table[16, first + 1]].astype(F32) * weight[0, first + 1]
                partial[k, offset + b] = total.astype(BF16)
                return carry

            return run

        row = (x // 2) * 4 * 2 * blocks
        lax.fori_loop(0, blocks, one(row + friend * 2 * blocks, blocks), 0)
        go(k, 18, partial.at[k, pl.ds(blocks, blocks)], final.at[k], mate)
        lax.fori_loop(0, blocks, one(row + me * 2 * blocks, 0), 0)

    def finish(k):
        arrived(k, 18)
        rows = slice(k * depth, (k + 1) * depth)

        def run(b, carry):
            total = base_ref[b, rows, :].astype(F32) + partial[k, b].astype(F32)
            total = total + final[k, b].astype(F32)
            for i in range(2):
                share = jnp.where(table[21, i] == b, weight[2, i], 0.0)
                total = total + hot_out[i, rows, :].astype(F32) * share
            out_ref[b, rows, :] = total.astype(BF16)
            return carry

        lax.fori_loop(0, blocks, run, 0)

    right, left = at(z, x + 1, c), at(z, x - 1, c)
    ring = ((x, right, left), (z, up, down))
    hot_made = {}

    def hot_go(n, src, dst, device):
        copy = remote(src, dst, hot_send.at[n], hot_recv.at[n], device)
        copy.start()
        pending.append(copy)
        hot_made[n] = copy

    short = SLICE // 2

    def hot_rows(order, spot, shift=0, size=SLICE):
        row = order * (HALF // 2) + ((spot + WAYS) % WAYS) * SLICE + shift
        return hotw.at[c, pl.ds(row, size)]

    def hot_begin(order, part):
        spot, plus, minus = ring[order]
        shift = part * short
        piece = slice_ref.at[order, pl.ds(shift, short)]
        there = hot_rows(order, spot, shift, short)
        base = 16 * order + 8 * part
        hot_go(base, piece, there, plus)
        hot_go(base + 1, piece, there, minus)
        hot_go(base + 2, piece, there, sibling)
        copy = pltpu.make_async_copy(piece, there, hot_local.at[2 * order + part])
        copy.start()
        hot_made["keep", order, part] = copy

    def hot_relay(order, part):
        spot, plus, minus = ring[order]
        base = 16 * order + 8 * part
        shift = part * short
        for n, neighbour in ((0, spot - 1), (1, spot + 1)):
            hot_made[base + n].wait_recv()
            there = hot_rows(order, neighbour, shift, short)
            if n == part:
                hot_go(base + 3, there, there, plus if n == 0 else minus)
            hot_go(base + 4 + n, there, there, sibling)

    def hot_last(order, part):
        spot = ring[order][0]
        base = 16 * order + 8 * part
        hot_made[base + 3].wait_recv()
        there = hot_rows(order, spot + 2, part * short, short)
        hot_go(base + 6, there, there, sibling)

    def hot_ready():
        for order in range(2):
            for part in range(2):
                hot_made["keep", order, part].wait()
                for n in (2, 4, 5, 6):
                    hot_made[16 * order + 8 * part + n].wait_recv()

    hidden = wg_ref.shape[1]
    def hot_first():
        rows = jnp.concatenate([f_ref[table[21, 0]], f_ref[table[21, 1]]], axis=0)
        low, high = rows[:, :HALF], rows[:, HALF:]

        def both(start):
            cols = slice(start, start + hidden)
            return jnp.dot(low, hotw[0, :, cols], preferred_element_type=F32) + jnp.dot(
                high, hotw[1, :, cols], preferred_element_type=F32
            )

        hot_inner[...] = (jax.nn.silu(both(0)) * both(hidden)).astype(BF16)

    def hot_second():
        cols = slice(2 * hidden, 2 * hidden + width)
        result = jnp.dot(hot_inner[:, :HALF], hotw[0, :, cols], preferred_element_type=F32)
        result = result + jnp.dot(
            hot_inner[:, HALF:], hotw[1, 2 * HALF - hidden :, cols], preferred_element_type=F32
        )
        hot_out[...] = result.astype(BF16).reshape(2, ROWS, width)

    stages = [widen, select, climb, forward, work, forward_back, give, mirror, build]
    begin(0)
    begin(1)
    hot_begin(1, 0)
    hot_begin(1, 1)
    extras = {
        2: ((hot_relay, 1, 0), (hot_begin, 0, 0)),
        3: ((hot_relay, 1, 1),),
        4: ((hot_last, 1, 0), (hot_relay, 0, 0)),
        5: ((hot_last, 1, 1), (hot_begin, 0, 1)),
        7: ((hot_last, 0, 0), (hot_relay, 0, 1)),
        9: ((hot_last, 0, 1),),
        chunks + 3: ((hot_ready,), (hot_first,)),
        chunks + 4: ((hot_second,),),
    }
    lag_of = len(stages)
    done = 0
    for step in range(chunks + lag_of):
        if step + 2 < chunks:
            begin(step + 2)
        for lag in reversed(range(lag_of)):
            if 0 <= step - lag < chunks:
                stages[lag](step - lag)
        for extra in extras.get(step, ()):
            extra[0](*extra[1:])
        if step > chunks + 4:
            while done <= min(step - lag_of, chunks - 1):
                finish(done)
                done += 1
    for copy in pending:
        copy.wait_send()


def moe(table, weight, ffn_in, base, w_gate, w_up, w_down, hot_slices):
    blocks, rows, width = ffn_in.shape
    packed = hot_slices.shape[2]
    chunks = CHUNKS
    depth = rows // chunks
    pair = 2 * CORES * blocks
    whole = pl.BlockSpec(memory_space=pltpu.VMEM)
    return pl.pallas_call(
        functools.partial(moe_kernel, blocks, chunks),
        out_shape=jax.ShapeDtypeStruct(base.shape, BF16),
        in_specs=[pl.BlockSpec(memory_space=pltpu.SMEM)] * 2 + [whole] * 6,
        out_specs=whole,
        scratch_shapes=[pltpu.VMEM((pair, depth, width), BF16)] * chunks
        + [pltpu.VMEM((CORES * 16, depth, width), BF16)] * chunks
        + [
            pltpu.VMEM((chunks, WAYS, SLOTS, depth, width), BF16),
            pltpu.VMEM((chunks, WAYS, SIDES, SLOTS, depth, width), BF16),
            pltpu.VMEM((chunks, SIDES, SLOTS, depth, width), BF16),
            pltpu.VMEM((chunks, WAYS, SIDES, SLOTS, depth, width), BF16),
            pltpu.VMEM((chunks, WAYS, SIDES, SLOTS, depth, width), BF16),
            pltpu.VMEM((chunks, SIDES, SLOTS, depth, width), BF16),
            pltpu.VMEM((chunks, WAYS * SLOTS, depth, width), BF16),
            pltpu.VMEM((chunks, 2 * blocks, depth, width), BF16),
            pltpu.VMEM((chunks, blocks, depth, width), BF16),
            pltpu.SemaphoreType.DMA((chunks, 4)),
            pltpu.SemaphoreType.DMA((chunks, 22)),
            pltpu.SemaphoreType.DMA((chunks, 22)),
            pltpu.VMEM((CORES, HALF, packed), BF16),
            pltpu.VMEM((2 * rows, w_gate.shape[1]), BF16),
            pltpu.VMEM((2, rows, width), BF16),
            pltpu.SemaphoreType.DMA((4,)),
            pltpu.SemaphoreType.DMA((32,)),
            pltpu.SemaphoreType.DMA((32,)),
        ],
        compiler_params=pltpu.CompilerParams(
            collective_id=1, has_side_effects=True, vmem_limit_bytes=67043328
        ),
        name="moe",
    )(table, weight, ffn_in, base, w_gate, w_up, w_down, hot_slices)


def tables_kernel(turn, int_ref, real_ref, out_int, out_real):
    out_int[...] = int_ref[...]
    out_real[...] = real_ref[...]
    out_real[2:3, :] = jnp.zeros((1, LANES), F32)
    tables(
        turn[0], int_ref[17:18, :], int_ref[18:19, :], real_ref[1:2, :], int_ref[19:20, :],
        out_int, out_real,
    )


def later_tables(turn, ints, reals):
    return pl.pallas_call(
        tables_kernel,
        out_shape=[
            jax.ShapeDtypeStruct(ints.shape, ints.dtype),
            jax.ShapeDtypeStruct(reals.shape, reals.dtype),
        ],
        in_specs=[pl.BlockSpec(memory_space=pltpu.SMEM)]
        + [pl.BlockSpec(memory_space=pltpu.VMEM)] * 2,
        out_specs=[pl.BlockSpec(memory_space=pltpu.VMEM)] * 2,
        name="later_tables",
    )(turn, ints, reals)


def body(
    hidden_in, attn_gain, w_qkv, head_gain, w_out, ffn_gain, w_gate, w_up, w_down, pair_ids, gate_codes
):
    tokens, width = hidden_in.shape
    blocks = tokens // ROWS
    groups = lax.axis_size("grp")
    weights = (w_gate[0], w_up[0], w_down[0])
    resid, ffn_in, ints, reals, hot_slices = front(
        hidden_in, attn_gain[None], w_qkv, head_gain[None], w_out, ffn_gain[None], *weights, pair_ids,
        gate_codes, groups,
    )
    resid = resid.reshape(blocks, ROWS, width)
    ffn_in = ffn_in.reshape(blocks, ROWS, width)

    def unfinished(carry):
        return carry[0] * SLOTS < carry[1][22, 0]

    def one(carry):
        turn, ints, reals, total = carry
        total = moe(ints, reals, ffn_in, total, *weights, hot_slices)
        turn = turn + 1
        ints, reals = lax.cond(
            turn * SLOTS < ints[22, 0],
            lambda pair: tuple(later_tables(turn[None], *pair)),
            lambda pair: pair,
            (ints, reals),
        )
        return turn, ints, reals, total

    total = lax.while_loop(unfinished, one, (jnp.int32(0), ints, reals, resid))[3]
    return total.reshape(tokens, width)


def solution(mesh):
    return jax.shard_map(
        body,
        mesh=mesh,
        in_specs=(
            P(("grp", "seq"), None), P(), P(), P(), P(), P(),
            P("seq", None, None), P("seq", None, None), P("seq", None, None),
            P(("grp", "seq"), None), P(("grp", "seq"), None),
        ),
        out_specs=P(("grp", "seq"), None),
        check_vma=False,
    )
```

profile of v0, /device:TPU:24, one launch (start us, length us, event | category | flops | bytes accessed | tf_op | source)
XLA Modules:
  0.0 220.7 jit_solution(3504209240298515511)
XLA Ops:
  0.0 1.4 copy.12.pairs
  1.4 1.3 copy.13.codes
  2.7 60.8 %front.1 = (bf16[896,1024]{1,0:T(8,128)(2,1)}, bf16[896,1024]{1,0:T(8,128)(2,1)}, s32[24,128]{1,0:T(8,128)}, f32[8,128]{1,0:T(8,128)S(1)}, bf16[2,64,2816]{2,1,0:T(8,128)(2,1)}) custom-call(s32[7,2]{1,0:T(8,128)} %copy.12.pairs, s32[7,2]{1,0:T(8,128)} %copy.13.codes, bf16[896,1024]{1,0:T(8,128)(2,1)} %x_ref.1, f32[1,1024]{1,0:T(1,128)} %bitcast.22, ...), custom_call_target="tpu_custom_call" | custom-call | tf_op jit(solution)/shard_map/front/pallas_call | solution.py:458
  63.5 154.3 %while.14 = (s32[]{:T(128)}, s32[24,128]{1,0:T(8,128)}, f32[8,128]{1,0:T(8,128)S(1)}, bf16[7,128,1024]{2,1,0:T(8,128)(2,1)}, bf16[7,128,1024]{2,1,0:T(8,128)(2,1...) while((s32[]{:T(128)}, s32[24,128]{1,0:T(8,128)}, ...), condition=%wide.region_3.0_spmd, body=%wide.region_0.0_spmd.sunk | while | flops 6 | bytes 3752191 | solution.py:864
  63.5 1.2 slice.6
  65.4 0.0 copy-start
  65.4 1.2 slice.8
  67.3 2.9 %copy.34.base_ref = bf16[7,128,1024]{2,1,0:T(8,128)(2,1)} copy(bf16[7,128,1024]{2,1,0:T(8,128)(2,1)} %get-tuple-element.175) | data formatting | bytes 3670016 | tf_op jit(solution)/shard_map/while
  70.2 0.0 copy-done
  70.2 1.9 conditional.2
  70.2 0.6 copy.15
  70.8 1.3 copy.14
  72.1 141.9 %moe.1 = bf16[7,128,1024]{2,1,0:T(8,128)(2,1)} custom-call(s32[24,128]{1,0:T(8,128)} %get-tuple-element.173.table, f32[8,128]{1,0:T(8,128)} %copy-done, bf16[7,128,1024]{2,1,0:T(8,128)(2,1)} %get-tuple-element.187.f_ref, bf16[7,128,1024]{2,1,0:T(8,128)(2,1)} %copy.34.base_ref, bf16[1024,896]{1,0:T(8,128)(2,1)} %get-tuple-element.188.wg_ref, ...), custom_call_target="tpu_custom_call" | custom-call | tf_op jit(solution)/shard_map/while/body/moe/pallas_call | solution.py:777
  214.0 0.7 copy.28
  214.7 1.3 copy.27
  216.0 1.2 slice.6
  217.8 2.9 %copy.35 = bf16[896,1024]{1,0:T(8,128)(2,1)} copy(bf16[896,1024]{1,0:T(8,128)(2,1)} %bitcast.11) | data formatting | bytes 3670016
Async XLA Ops:
  65.4 4.8 %copy-start = (f32[8,128]{1,0:T(8,128)}, f32[8,128]{1,0:T(8,128)S(1)}, u32[]{:S(2)}) copy-start(f32[8,128]{1,0:T(8,128)S(1)} %get-tuple-element.174.weight) | copy-start | bytes 12292 | tf_op jit(solution)/shard_map/while
where the time goes:
time: 223 us; the launch traced here: 221 us
  Pallas kernels  203 us (91%)
  local copies, waits for them, and re-layouts  16 us (7%)
    pallas_call x1, Pallas kernels, moe(): pl.pallas_call(functools.partial(moe_kernel, blocks, chunks), out_shape=j...  142 us
    pallas_call x1, Pallas kernels, front(): pl.pallas_call(functools.partial(front_kernel, groups, blocks), out_shape...  60.8 us
    unnamed x3, local copies, waits for them, and re-layouts  5.56 us
    while x5, local copies, waits for them, and re-layouts  4.93 us

commit v1 on v0

--- a/solution.py
+++ b/solution.py
@@ -21,6 +21,7 @@
 LIMIT = 8
 LANES = 128
 HALF = 512
+TILE = 256
 SLICE = 64
 PIECE = 16
 HOT = 15
@@ -103,6 +104,7 @@
     tiles = tokens // ROWS
     step = 2 * HEAD_DIM
     steps = width // step
+    half = tokens // 2
 
     def at(yy, zz, xx, cc):
         return (yy, zz * lane_count + xx * CORES + cc)
@@ -226,10 +228,14 @@
     first = (x * CORES + c) * visits
     info = jnp.zeros((8, LANES), jnp.int32)
     for b in range(blocks):
-        both = codes[b, 0] + codes[b, 1]
+        code = codes[:, b : b + 1]
+        pair = pairs[:, b : b + 1] + 1
+        both = code[0:1, :] + code[1:2, :]
         for j in range(2):
             here = lane == first + (2 * b + j)
-            value = jnp.where(sub == 0, pairs[b, j] + 1, jnp.where(sub == 1, codes[b, j], both))
+            value = jnp.where(
+                sub == 0, pair[j : j + 1, :], jnp.where(sub == 1, code[j : j + 1, :], both)
+            )
             info = jnp.where(here & (sub < 3), value, info)
     chip[...] = info
     waits = [go(chip, sib, sibling)]
@@ -247,11 +253,17 @@
         for part in range(3):
             fetches[part * steps + j].wait()
         cols = slice(j * step, (j + 1) * step)
-        q[:, cols] = lifted(jnp.dot(normed[...], wcols[j], preferred_element_type=F32))
-        k[:, cols] = lifted(jnp.dot(normed[...], wcols[steps + j], preferred_element_type=F32))
-        v[:, cols] = jnp.dot(
-            normed[...], wcols[2 * steps + j], preferred_element_type=F32
-        ).astype(BF16)
+
+        @pl.loop(0, 2)
+        def _(i):
+            part = pl.ds(pl.multiple_of(i * half, PIECE), half)
+            rows_in = normed[part, :]
+            q[part, cols] = lifted(jnp.dot(rows_in, wcols[j], preferred_element_type=F32))
+            k[part, cols] = lifted(jnp.dot(rows_in, wcols[steps + j], preferred_element_type=F32))
+            v[part, cols] = jnp.dot(
+                rows_in, wcols[2 * steps + j], preferred_element_type=F32
+            ).astype(BF16)
+
         for head in range(2 * j, 2 * j + 2):
             cols = slice(head * HEAD_DIM, (head + 1) * HEAD_DIM)
             keys = k[:, cols]
@@ -419,9 +431,10 @@
     reduce_waits = gather_pieces(reduce_waits)
     arrive(waits)
     add_prior((1 - c) * WAYS, sib2)
-    half = tokens // 2
-    for part in range(2):
-        part_rows = slice(part * half, (part + 1) * half)
+
+    @pl.loop(0, 2)
+    def _(part):
+        part_rows = pl.ds(pl.multiple_of(part * half, PIECE), half)
         attended = norm_rows(ratio[part_rows, :], hgain_ref[...]).astype(BF16)
         resid = x_ref[part_rows, :].astype(F32) + jnp.dot(
             attended, wout_ref[...], preferred_element_type=F32
@@ -439,7 +452,7 @@
 ):
     tokens, width = x.shape
     packed = 2 * w_gate.shape[1] + width
-    blocks = pair_ids.shape[0]
+    blocks = pair_ids.shape[1]
     tile = (8, LANES)
     one = (STATE, HEAD_DIM)
     some = (WAYS,) + one
@@ -452,7 +465,6 @@
     def wide(*shape):
         return pltpu.VMEM(shape + (packed,), BF16)
 
-    smem = pl.BlockSpec(memory_space=pltpu.SMEM)
     vmem = pl.BlockSpec(memory_space=pltpu.VMEM)
     hbm = pl.BlockSpec(memory_space=pl.ANY)
     return pl.pallas_call(
@@ -460,7 +472,7 @@
         out_shape=[jax.ShapeDtypeStruct((tokens, width), BF16)] * 2
         + [jax.ShapeDtypeStruct((24, LANES), jnp.int32), jax.ShapeDtypeStruct(tile, F32)]
         + [jax.ShapeDtypeStruct((2, SLICE, packed), BF16)],
-        in_specs=[smem] * 2 + [vmem] * 2 + [hbm] + [vmem] * 3 + [hbm] * 3,
+        in_specs=[vmem] * 4 + [hbm] + [vmem] * 3 + [hbm] * 3,
         out_specs=[vmem] * 5,
         scratch_shapes=[pltpu.VMEM((tokens, width), BF16)] * 4
         + [pltpu.VMEM((pieces, width, step), BF16), pltpu.VMEM(every, F32)]
@@ -510,10 +522,11 @@
     gather, landed = rest[:chunks], rest[chunks : 2 * chunks]
     (
         hand, zs, relay, taken, made_rows, relay_back, hand_back, partial, final, local, send, recv,
-        hotw, hot_inner, hot_out, hot_local, hot_send, hot_recv,
+        inside, hotw, hot_inner, hot_out, hot_local, hot_send, hot_recv,
     ) = rest[2 * chunks :]
     depth = ROWS // chunks
     width = f_ref.shape[2]
+    hidden = wg_ref.shape[1]
     y, z, x, c = place()
     lane = WAYS * CORES
     parity = x % 2
@@ -589,12 +602,27 @@
     def work(k):
         arrived(k, 4, 5, 7, 20)
         made[k, "keep", 1].wait()
-        rows = taken[k].reshape(WAYS * PART * depth, width)
-        gate = jnp.dot(rows, wg_ref[...], preferred_element_type=F32)
-        upper = jnp.dot(rows, wu_ref[...], preferred_element_type=F32)
-        inner = (jax.nn.silu(gate) * upper).astype(BF16)
-        result = jnp.dot(inner, wd_ref[...], preferred_element_type=F32).astype(BF16)
-        made_rows[k] = result.reshape(WAYS, SIDES, SLOTS, depth, width)
+        def rise(cols):
+            rows = taken[k].reshape(WAYS * PART * depth, width)
+            gate = jnp.dot(rows, wg_ref[:, cols], preferred_element_type=F32)
+            upper = jnp.dot(rows, wu_ref[:, cols], preferred_element_type=F32)
+            inside[:, cols] = (jax.nn.silu(gate) * upper).astype(BF16)
+
+        @pl.loop(0, hidden // TILE)
+        def _(i):
+            rise(pl.ds(pl.multiple_of(i * TILE, TILE), TILE))
+
+        if hidden % TILE:
+            rise(slice(hidden - hidden % TILE, hidden))
+
+        @pl.loop(0, width // TILE)
+        def _(i):
+            cols = pl.ds(pl.multiple_of(i * TILE, TILE), TILE)
+            result = jnp.dot(inside[...], wd_ref[:, cols], preferred_element_type=F32)
+            made_rows[k, :, :, :, :, cols] = result.astype(BF16).reshape(
+                WAYS, SIDES, SLOTS, depth, TILE
+            )
+
         go(k, 12, made_rows.at[k, step_of(z + 2), 0], relay_back.at[k, 0], up)
         go(k, 21, made_rows.at[k, step_of(z + 2), 1], relay_back.at[k, 1], down)
         for n, d, device in ((8, 1, up), (10, -1, down)):
@@ -713,26 +741,34 @@
                 for n in (2, 4, 5, 6):
                     hot_made[16 * order + 8 * part + n].wait_recv()
 
-    hidden = wg_ref.shape[1]
     def hot_first():
-        rows = jnp.concatenate([f_ref[table[21, 0]], f_ref[table[21, 1]]], axis=0)
-        low, high = rows[:, :HALF], rows[:, HALF:]
-
-        def both(start):
-            cols = slice(start, start + hidden)
-            return jnp.dot(low, hotw[0, :, cols], preferred_element_type=F32) + jnp.dot(
-                high, hotw[1, :, cols], preferred_element_type=F32
+        def rise(start):
+            rows = jnp.concatenate([f_ref[table[21, 0]], f_ref[table[21, 1]]], axis=0)
+            low, high = rows[:, :HALF], rows[:, HALF:]
+
+            def both(cols):
+                return jnp.dot(low, hotw[0, :, cols], preferred_element_type=F32) + jnp.dot(
+                    high, hotw[1, :, cols], preferred_element_type=F32
+                )
+
+            gate = both(pl.ds(start, HEAD_DIM))
+            upper = both(pl.ds(pl.multiple_of(start + hidden, HEAD_DIM), HEAD_DIM))
+            hot_inner[:, pl.ds(start, HEAD_DIM)] = (jax.nn.silu(gate) * upper).astype(BF16)
+
+        @pl.loop(0, hidden // HEAD_DIM)
+        def _(i):
+            rise(pl.multiple_of(i * HEAD_DIM, HEAD_DIM))
+
+    def hot_second():
+        @pl.loop(0, width // TILE)
+        def _(i):
+            start = pl.multiple_of(i * TILE, TILE)
+            cols = pl.ds(pl.multiple_of(2 * hidden + start, TILE), TILE)
+            result = jnp.dot(hot_inner[:, :HALF], hotw[0, :, cols], preferred_element_type=F32)
+            result = result + jnp.dot(
+                hot_inner[:, HALF:], hotw[1, 2 * HALF - hidden :, cols], preferred_element_type=F32
             )
-
-        hot_inner[...] = (jax.nn.silu(both(0)) * both(hidden)).astype(BF16)
-
-    def hot_second():
-        cols = slice(2 * hidden, 2 * hidden + width)
-        result = jnp.dot(hot_inner[:, :HALF], hotw[0, :, cols], preferred_element_type=F32)
-        result = result + jnp.dot(
-            hot_inner[:, HALF:], hotw[1, 2 * HALF - hidden :, cols], preferred_element_type=F32
-        )
-        hot_out[...] = result.astype(BF16).reshape(2, ROWS, width)
+            hot_out[:, :, pl.ds(start, TILE)] = result.astype(BF16).reshape(2, ROWS, TILE)
 
     stages = [widen, select, climb, forward, work, forward_back, give, mirror, build]
     begin(0)
@@ -794,6 +830,7 @@
             pltpu.SemaphoreType.DMA((chunks, 4)),
             pltpu.SemaphoreType.DMA((chunks, 22)),
             pltpu.SemaphoreType.DMA((chunks, 22)),
+            pltpu.VMEM((WAYS * PART * depth, w_gate.shape[1]), BF16),
             pltpu.VMEM((CORES, HALF, packed), BF16),
             pltpu.VMEM((2 * rows, w_gate.shape[1]), BF16),
             pltpu.VMEM((2, rows, width), BF16),
@@ -840,28 +877,22 @@
     groups = lax.axis_size("grp")
     weights = (w_gate[0], w_up[0], w_down[0])
     resid, ffn_in, ints, reals, hot_slices = front(
-        hidden_in, attn_gain[None], w_qkv, head_gain[None], w_out, ffn_gain[None], *weights, pair_ids,
-        gate_codes, groups,
+        hidden_in, attn_gain[None], w_qkv, head_gain[None], w_out, ffn_gain[None], *weights, pair_ids.T,
+        gate_codes.T, groups,
     )
     resid = resid.reshape(blocks, ROWS, width)
     ffn_in = ffn_in.reshape(blocks, ROWS, width)
 
-    def unfinished(carry):
-        return carry[0] * SLOTS < carry[1][22, 0]
-
-    def one(carry):
-        turn, ints, reals, total = carry
-        total = moe(ints, reals, ffn_in, total, *weights, hot_slices)
-        turn = turn + 1
-        ints, reals = lax.cond(
-            turn * SLOTS < ints[22, 0],
-            lambda pair: tuple(later_tables(turn[None], *pair)),
-            lambda pair: pair,
-            (ints, reals),
-        )
-        return turn, ints, reals, total
-
-    total = lax.while_loop(unfinished, one, (jnp.int32(0), ints, reals, resid))[3]
+    total = moe(ints, reals, ffn_in, resid, *weights, hot_slices)
+
+    def more(total):
+        def one(turn, total):
+            later_ints, later_reals = later_tables(turn[None], ints, reals)
+            return moe(later_ints, later_reals, ffn_in, total, *weights, hot_slices)
+
+        return lax.fori_loop(1, -(-LIMIT // SLOTS), one, total)
+
+    total = lax.cond(ints[22, 0] > SLOTS, more, lambda total: total, total)
     return total.reshape(tokens, width)
 
 

time: 223 us -> 213 us (0.955)
  local copies, waits for them, and re-layouts: 16 us -> 4.04 us
    while x5 -> x0, local copies, waits for them, and re-layouts: 4.93 us -> none
    pallas_call x1, Pallas kernels: 142 us -> 146 us  [moe(): pl.pallas_call(functools.partial(moe_kernel, blocks, chunks), out_shape=j...]
    slice x3 -> x1, local copies, waits for them, and re-layouts: 3.59 us -> 0.58 us  [body(): total = lax.cond(ints[22, 0] > SLOTS, more, lambda total: total, total)]
where the time goes in v1:
time: 213 us; the launch traced here: 210 us
  Pallas kernels  205 us (96%)
  local copies, waits for them, and re-layouts  4.04 us (2%)
    pallas_call x1, Pallas kernels, moe(): pl.pallas_call(functools.partial(moe_kernel, blocks, chunks), out_shape=j...  146 us
    pallas_call x1, Pallas kernels, front(): pl.pallas_call(functools.partial(front_kernel, groups, blocks), out_shape...  58.8 us

profile of v1, /device:TPU:24, one launch (start us, length us, event | category | flops | bytes accessed | tf_op | source)
XLA Modules:
  0.0 209.9 jit_solution(1158183056298687136)
XLA Ops:
  0.0 58.8 %front.1 = (bf16[896,1024]{1,0:T(8,128)(2,1)}, bf16[896,1024]{1,0:T(8,128)(2,1)}, s32[24,128]{1,0:T(8,128)S(1)}, f32[8,128]{1,0:T(8,128)}, bf16[2,64,2816]{2,1,0:T(8,128)(2,1)}) custom-call(s32[2,7]{1,0:T(2,128)} %bitcast.33, s32[2,7]{1,0:T(2,128)} %bitcast.34, bf16[896,1024]{1,0:T(8,128)(2,1)} %x_ref.1, f32[1,1024]{1,0:T(1,128)} %bitcast.30, ...), custom_call_target="tpu_custom_call" | custom-call | tf_op jit(solution)/shard_map/front/pallas_call | solution.py:470
  58.8 0.0 copy-start
  58.8 0.6 copy-done
  59.4 0.6 slice.3
  60.6 146.4 %moe.6 = bf16[7,128,1024]{2,1,0:T(8,128)(2,1)} custom-call(s32[24,128]{1,0:T(8,128)} %copy-done, f32[8,128]{1,0:T(8,128)} %get-tuple-element.295.weight, bf16[7,128,1024]{2,1,0:T(8,128)(2,1)} %bitcast.27, bf16[7,128,1024]{2,1,0:T(8,128)(2,1)} %bitcast.29, bf16[1024,896]{1,0:T(8,128)(2,1)} %bitcast.19, bf16[1024,896]{1,0:T(8,128)(2,1)} %bitcast.22, ...), custom_call_target="tpu_custom_call" | custom-call | tf_op jit(solution)/shard_map/moe/pallas_call | solution.py:813
  207.0 2.9 %copy.26 = bf16[896,1024]{1,0:T(8,128)(2,1)} copy(bf16[896,1024]{1,0:T(8,128)(2,1)} %get-tuple-element.184) | data formatting | bytes 3670016
  (1 shorter events, 0.0 us)
Async XLA Ops:
  58.8 0.6 copy-start

commit v2 on v1

--- a/solution.py
+++ b/solution.py
@@ -155,72 +155,62 @@
         local.start()
         fetches.append(local)
 
-    def start_reduce(far_half):
-        waits = []
-        for order, (spot, plus, minus, _) in enumerate(ring):
-            top = order * (HALF // 2)
-
-            def part(i, shift=0, size=SLICE):
-                row = top + ((spot + i + WAYS) % WAYS) * SLICE + shift
-                return near.at[pl.ds(row, size)]
-
-            short = SLICE // 2
-            if far_half:
-                waits.append(
-                    (
-                        go(part(2, 0, short), halves_in.at[order, 0], plus),
-                        go(part(2, short, short), halves_in.at[order, 1], minus),
-                    )
-                )
-            else:
-                waits.append(
-                    (
-                        go(part(1), slices.at[order, 0], plus),
-                        go(part(-1), slices.at[order, 1], minus),
-                    )
-                )
-        return waits
-
-    def relay_reduce(waits):
-        short = SLICE // 2
-        for order, (_, plus, minus, _) in enumerate(ring):
-            arrive(waits[order])
-            waits[order] = (
-                go(halves_in.at[order, 0], slices.at[order, 2, pl.ds(0, short)], plus),
-                go(halves_in.at[order, 1], slices.at[order, 2, pl.ds(short, short)], minus),
+    short = SLICE // 2
+    held = {}
+
+    def part_of(order, i, shift=0, size=SLICE):
+        row = order * (HALF // 2) + ((ring[order][0] + i + WAYS) % WAYS) * SLICE + shift
+        return near.at[pl.ds(row, size)]
+
+    def send_near(order):
+        _, plus, minus, _ = ring[order]
+        held[order, 0] = go(part_of(order, 1), slices.at[order, 0], plus)
+        held[order, 1] = go(part_of(order, -1), slices.at[order, 1], minus)
+
+    def send_far(order):
+        _, plus, minus, _ = ring[order]
+        held[order, 2] = go(part_of(order, 2, 0, short), halves_in.at[order, 0], plus)
+        held[order, 3] = go(part_of(order, 2, short, short), halves_in.at[order, 1], minus)
+
+    def relay_far(order):
+        _, plus, minus, _ = ring[order]
+        arrive([held[order, 2], held[order, 3]])
+        first_half, second_half = slices.at[order, 2, pl.ds(0, short)], slices.at[order, 2, pl.ds(short, short)]
+        held[order, 4] = go(halves_in.at[order, 0], first_half, plus)
+        held[order, 5] = go(halves_in.at[order, 1], second_half, minus)
+
+    def second_reduce(order):
+        arrive([held[order, n] for n in (0, 1, 4, 5)])
+        top = order * (HALF // 2) + ring[order][0] * SLICE
+
+        @pl.loop(0, SLICE // PIECE)
+        def _(i):
+            row = pl.multiple_of(i * PIECE, PIECE)
+            base_rows = pl.ds(pl.multiple_of(top + row, PIECE), PIECE)
+            row = pl.ds(row, PIECE)
+            total = near[base_rows, :] + slices[order, 0, row, :]
+            summed[order, row, :] = total + (slices[order, 1, row, :] + slices[order, 2, row, :])
+
+        spot, plus, minus, opposite = ring[1 - order]
+        held[order, "pieces"] = [
+            go(
+                summed.at[order, pl.ds(((spot + d) % WAYS) * PIECE, PIECE)],
+                pieces_in.at[order, d - 1],
+                device,
             )
-
-    def second_reduce(waits):
-        later = []
-        for order, (spot, _, _, _) in enumerate(ring):
-            arrive(waits[order])
-            top = order * (HALF // 2) + spot * SLICE
-
-            @pl.loop(0, SLICE // PIECE)
-            def _(i):
-                row = pl.multiple_of(i * PIECE, PIECE)
-                base_rows = pl.ds(pl.multiple_of(top + row, PIECE), PIECE)
-                row = pl.ds(row, PIECE)
-                total = near[base_rows, :] + slices[order, 0, row, :]
-                summed[order, row, :] = total + (slices[order, 1, row, :] + slices[order, 2, row, :])
-
-            spot, plus, minus, opposite = ring[1 - order]
-            for d, device in ((1, plus), (2, opposite), (3, minus)):
-                piece = summed.at[order, pl.ds(((spot + d) % WAYS) * PIECE, PIECE)]
-                later.append(go(piece, pieces_in.at[order, d - 1], device))
-        return later
-
-    def gather_pieces(waits):
-        arrive(waits)
-        later = []
-        for order in range(2):
-            spot, plus, minus, opposite = ring[1 - order]
-            row = pl.ds(pl.multiple_of(spot * PIECE, PIECE), PIECE)
-            total = summed[order, row, :] + pieces_in[order, 0]
-            hot_ref[order, row, :] = total + (pieces_in[order, 1] + pieces_in[order, 2])
-            for device in (plus, opposite, minus):
-                later.append(go(hot_ref.at[order, row], hot_ref.at[order, row], device))
-        return later
+            for d, device in ((2, opposite), (1, plus), (3, minus))
+        ]
+
+    def gather_pieces(order):
+        arrive(held[order, "pieces"])
+        spot, plus, minus, opposite = ring[1 - order]
+        row = pl.ds(pl.multiple_of(spot * PIECE, PIECE), PIECE)
+        total = summed[order, row, :] + pieces_in[order, 0]
+        hot_ref[order, row, :] = total + (pieces_in[order, 1] + pieces_in[order, 2])
+        return [
+            go(hot_ref.at[order, row], hot_ref.at[order, row], device)
+            for device in (opposite, plus, minus)
+        ]
 
     visits = 2 * blocks
     lane = lax.broadcasted_iota(jnp.int32, (8, LANES), 1)
@@ -249,8 +239,17 @@
     chips[x] = info + sib[...]
     waits = [go(chips.at[x], chips.at[x], device) for device in along_x]
 
+    def project_query(j):
+        fetches[j].wait()
+        cols = slice(j * step, (j + 1) * step)
+
+        @pl.loop(0, 2)
+        def _(i):
+            part = pl.ds(pl.multiple_of(i * half, PIECE), half)
+            q[part, cols] = lifted(jnp.dot(normed[part, :], wcols[j], preferred_element_type=F32))
+
     def project(j):
-        for part in range(3):
+        for part in range(1, 3):
             fetches[part * steps + j].wait()
         cols = slice(j * step, (j + 1) * step)
 
@@ -258,7 +257,6 @@
         def _(i):
             part = pl.ds(pl.multiple_of(i * half, PIECE), half)
             rows_in = normed[part, :]
-            q[part, cols] = lifted(jnp.dot(rows_in, wcols[j], preferred_element_type=F32))
             k[part, cols] = lifted(jnp.dot(rows_in, wcols[steps + j], preferred_element_type=F32))
             v[part, cols] = jnp.dot(
                 rows_in, wcols[2 * steps + j], preferred_element_type=F32
@@ -309,9 +307,11 @@
         row = pl.ds(pl.multiple_of(i * PIECE, PIECE), PIECE)
         near[row, :] = near[row, :] * here + far[row, :] * beside
 
-    reduce_waits = start_reduce(False)
+    send_near(1)
     project(3)
     waits = [go(mine, theirs, sibling)]
+    project_query(0)
+    project_query(1)
     hot = jnp.broadcast_to(hot, (1, LANES)).astype(jnp.int32)
     ids = info_row[0:1, :] - 1
     wide = jnp.broadcast_to(ids, (LANES, LANES))
@@ -377,28 +377,29 @@
                 numer[part, cols] = total[:, :HEAD_DIM]
                 denom[part, cols] = total[:, HEAD_DIM:]
 
-    within(0, 2)
     arrive(waits)
     base = c * WAYS
     for i in range(WAYS):
         sums[i] = (state[base + i] + theirs[base + i].astype(F32)).astype(BF16)
     xs[x] = sums[x]
     waits = [go(sums.at[(x + d) % WAYS], xs.at[x], along_x[d - 1]) for d in range(1, WAYS)]
-    far_waits = start_reduce(True)
-    within(2, 4)
+    send_near(0)
+    project_query(2)
+    project_query(3)
     arrive(waits)
     row_sum[...] = sum(xs[i].astype(F32) for i in range(WAYS)).astype(BF16)
     zs[z] = row_sum[...]
     waits = [go(row_sum, zs.at[z], along_z[d - 1]) for d in range(1, WAYS)]
-    relay_reduce(far_waits)
-    within(4, 6)
+    send_far(1)
+    within(0, 3)
     arrive(waits)
     plane_sum[...] = sum(zs[i].astype(F32) for i in range(WAYS)).astype(BF16)
     waits = [go(plane_sum, ys.at[y], along_y[d - 1]) for d in range(1, groups)]
     total = jnp.zeros(row_sum.shape, F32)
     for i in range(WAYS):
         total = total + zs[i].astype(F32) * jnp.where(i < z, 1.0, 0.0)
-    within(6, 7)
+    within(3, 6)
+    relay_far(1)
     arrive(waits)
     ys[y] = plane_sum[...]
     for i in range(groups):
@@ -408,8 +409,8 @@
         total = total + xs[i].astype(F32)
     heads_in[x] = back[x]
     waits = [go(back.at[(x + d) % WAYS], heads_in.at[x], along_x[d - 1]) for d in range(1, WAYS)]
-    within(7, 8)
-    reduce_waits = second_reduce([a + b for a, b in zip(reduce_waits, far_waits)])
+    send_far(0)
+    within(6, 8)
     arrive(waits)
     waits = [go(heads_in, sib2, sibling)]
     later = jnp.where(c == 1, 1.0, 0.0)
@@ -427,10 +428,13 @@
                 denom[:, cols] + total[:, HEAD_DIM:]
             )
 
+    second_reduce(1)
     add_prior(base, heads_in)
-    reduce_waits = gather_pieces(reduce_waits)
+    relay_far(0)
     arrive(waits)
     add_prior((1 - c) * WAYS, sib2)
+    reduce_waits = gather_pieces(1)
+    second_reduce(0)
 
     @pl.loop(0, 2)
     def _(part):
@@ -442,7 +446,7 @@
         resid = resid.astype(BF16)
         resid_ref[part_rows, :] = resid
         ffn_ref[part_rows, :] = norm_rows(resid.astype(F32), fgain_ref[...]).astype(BF16)
-    arrive(reduce_waits)
+    arrive(reduce_waits + gather_pieces(0))
     for copy in copies:
         copy.wait_send()
 
@@ -516,13 +520,13 @@
 
 
 def moe_kernel(
-    blocks, chunks, table, weight, f_ref, base_ref, wg_ref, wu_ref, wd_ref, slice_ref, out_ref,
+    blocks, chunks, table, weight, f_ref, base_hbm, wg_hbm, wu_hbm, wd_hbm, slice_ref, out_ref,
     *rest
 ):
     gather, landed = rest[:chunks], rest[chunks : 2 * chunks]
     (
         hand, zs, relay, taken, made_rows, relay_back, hand_back, partial, final, local, send, recv,
-        inside, hotw, hot_inner, hot_out, hot_local, hot_send, hot_recv,
+        base_ref, wg_ref, wu_ref, wd_ref, fetch_sem, inside, hotw, hot_inner, hot_out, hot_local, hot_send, hot_recv,
     ) = rest[2 * chunks :]
     depth = ROWS // chunks
     width = f_ref.shape[2]
@@ -538,6 +542,13 @@
     mate = at(z, x + 1 - 2 * parity, c)
     across = at(z, x + 2 * parity - 1, c)
     up, down = at(z + 1, x, c), at(z - 1, x, c)
+    fetched = []
+    for n, (source, place_in) in enumerate(
+        ((wg_hbm, wg_ref), (wu_hbm, wu_ref), (wd_hbm, wd_ref), (base_hbm, base_ref))
+    ):
+        fetch = pltpu.make_async_copy(source, place_in, fetch_sem.at[n])
+        fetch.start()
+        fetched.append(fetch)
     greet([sibling, mate, across, up, down])
     me = parity * CORES + c
     friend = (1 - parity) * CORES + c
@@ -600,6 +611,9 @@
         go(k, 20, relay.at[k, 1], taken.at[k, step_of(z + 1), 1], down)
 
     def work(k):
+        if k == 0:
+            for fetch in fetched:
+                fetch.wait()
         arrived(k, 4, 5, 7, 20)
         made[k, "keep", 1].wait()
         def rise(cols):
@@ -810,10 +824,11 @@
     depth = rows // chunks
     pair = 2 * CORES * blocks
     whole = pl.BlockSpec(memory_space=pltpu.VMEM)
+    hbm = pl.BlockSpec(memory_space=pl.ANY)
     return pl.pallas_call(
         functools.partial(moe_kernel, blocks, chunks),
         out_shape=jax.ShapeDtypeStruct(base.shape, BF16),
-        in_specs=[pl.BlockSpec(memory_space=pltpu.SMEM)] * 2 + [whole] * 6,
+        in_specs=[pl.BlockSpec(memory_space=pltpu.SMEM)] * 2 + [whole] + [hbm] * 4 + [whole],
         out_specs=whole,
         scratch_shapes=[pltpu.VMEM((pair, depth, width), BF16)] * chunks
         + [pltpu.VMEM((CORES * 16, depth, width), BF16)] * chunks
@@ -830,6 +845,11 @@
             pltpu.SemaphoreType.DMA((chunks, 4)),
             pltpu.SemaphoreType.DMA((chunks, 22)),
             pltpu.SemaphoreType.DMA((chunks, 22)),
+            pltpu.VMEM(base.shape, BF16),
+            pltpu.VMEM(w_gate.shape, BF16),
+            pltpu.VMEM(w_up.shape, BF16),
+            pltpu.VMEM(w_down.shape, BF16),
+            pltpu.SemaphoreType.DMA((4,)),
             pltpu.VMEM((WAYS * PART * depth, w_gate.shape[1]), BF16),
             pltpu.VMEM((CORES, HALF, packed), BF16),
             pltpu.VMEM((2 * rows, w_gate.shape[1]), BF16),

time: 213 us -> 221 us (1.038)
  Pallas kernels: 205 us -> 213 us
    pallas_call x1, Pallas kernels: 58.8 us -> 68.4 us  [front(): pl.pallas_call(functools.partial(front_kernel, groups, blocks), out_shape...]
where the time goes in v2:
time: 221 us; the launch traced here: 218 us
  Pallas kernels  213 us (96%)
  local copies, waits for them, and re-layouts  4.04 us (2%)
    pallas_call x1, Pallas kernels, moe(): pl.pallas_call(functools.partial(moe_kernel, blocks, chunks), out_shape=j...  144 us
    pallas_call x1, Pallas kernels, front(): pl.pallas_call(functools.partial(front_kernel, groups, blocks), out_shape...  68.4 us

profile of v2, /device:TPU:24, one launch (start us, length us, event | category | flops | bytes accessed | tf_op | source)
XLA Modules:
  0.0 217.6 jit_solution(797554393500912949)
XLA Ops:
  0.0 68.4 %front.1 = (bf16[896,1024]{1,0:T(8,128)(2,1)}, bf16[896,1024]{1,0:T(8,128)(2,1)}, s32[24,128]{1,0:T(8,128)S(1)}, f32[8,128]{1,0:T(8,128)}, bf16[2,64,2816]{2,1,0:T(8,128)(2,1)}) custom-call(s32[2,7]{1,0:T(2,128)} %bitcast.33, s32[2,7]{1,0:T(2,128)} %bitcast.34, bf16[896,1024]{1,0:T(8,128)(2,1)} %x_ref.1, f32[1,1024]{1,0:T(1,128)} %bitcast.30, ...), custom_call_target="tpu_custom_call" | custom-call | tf_op jit(solution)/shard_map/front/pallas_call | solution.py:474
  68.5 0.0 copy-start
  68.5 0.6 copy-done
  69.1 0.6 slice.3
  70.3 144.5 %moe.6 = bf16[7,128,1024]{2,1,0:T(8,128)(2,1)} custom-call(s32[24,128]{1,0:T(8,128)} %copy-done, f32[8,128]{1,0:T(8,128)} %get-tuple-element.295.weight, bf16[7,128,1024]{2,1,0:T(8,128)(2,1)} %bitcast.27, bf16[7,128,1024]{2,1,0:T(8,128)(2,1)} %bitcast.29, bf16[1024,896]{1,0:T(8,128)(2,1)} %bitcast.19, bf16[1024,896]{1,0:T(8,128)(2,1)} %bitcast.22, ...), custom_call_target="tpu_custom_call" | custom-call | tf_op jit(solution)/shard_map/moe/pallas_call | solution.py:828
  214.7 2.9 %copy.26 = bf16[896,1024]{1,0:T(8,128)(2,1)} copy(bf16[896,1024]{1,0:T(8,128)(2,1)} %get-tuple-element.184) | data formatting | bytes 3670016
  (1 shorter events, 0.0 us)
Async XLA Ops:
  68.5 0.6 copy-start

commit v3 on v2

--- a/solution.py
+++ b/solution.py
@@ -96,7 +96,7 @@
     normed, q, k, v, wcols, state, ratio, numer, denom,
     chip, chips, sib, rows, peak, peaks,
     mine, theirs, sums, xs, row_sum, zs, plane_sum, ys, back, heads_in, sib2,
-    near, far, slices, halves_in, summed, pieces_in, loads, stay, send, recv,
+    near, far, slices, halves_in, loads, stay, send, recv,
 ):
     y, z, x, c = place()
     lane_count = WAYS * CORES
@@ -189,28 +189,7 @@
             base_rows = pl.ds(pl.multiple_of(top + row, PIECE), PIECE)
             row = pl.ds(row, PIECE)
             total = near[base_rows, :] + slices[order, 0, row, :]
-            summed[order, row, :] = total + (slices[order, 1, row, :] + slices[order, 2, row, :])
-
-        spot, plus, minus, opposite = ring[1 - order]
-        held[order, "pieces"] = [
-            go(
-                summed.at[order, pl.ds(((spot + d) % WAYS) * PIECE, PIECE)],
-                pieces_in.at[order, d - 1],
-                device,
-            )
-            for d, device in ((2, opposite), (1, plus), (3, minus))
-        ]
-
-    def gather_pieces(order):
-        arrive(held[order, "pieces"])
-        spot, plus, minus, opposite = ring[1 - order]
-        row = pl.ds(pl.multiple_of(spot * PIECE, PIECE), PIECE)
-        total = summed[order, row, :] + pieces_in[order, 0]
-        hot_ref[order, row, :] = total + (pieces_in[order, 1] + pieces_in[order, 2])
-        return [
-            go(hot_ref.at[order, row], hot_ref.at[order, row], device)
-            for device in (opposite, plus, minus)
-        ]
+            hot_ref[order, row, :] = total + (slices[order, 1, row, :] + slices[order, 2, row, :])
 
     visits = 2 * blocks
     lane = lax.broadcasted_iota(jnp.int32, (8, LANES), 1)
@@ -307,6 +286,7 @@
         row = pl.ds(pl.multiple_of(i * PIECE, PIECE), PIECE)
         near[row, :] = near[row, :] * here + far[row, :] * beside
 
+    send_near(0)
     send_near(1)
     project(3)
     waits = [go(mine, theirs, sibling)]
@@ -383,14 +363,16 @@
         sums[i] = (state[base + i] + theirs[base + i].astype(F32)).astype(BF16)
     xs[x] = sums[x]
     waits = [go(sums.at[(x + d) % WAYS], xs.at[x], along_x[d - 1]) for d in range(1, WAYS)]
-    send_near(0)
+    send_far(0)
+    send_far(1)
     project_query(2)
     project_query(3)
     arrive(waits)
     row_sum[...] = sum(xs[i].astype(F32) for i in range(WAYS)).astype(BF16)
     zs[z] = row_sum[...]
     waits = [go(row_sum, zs.at[z], along_z[d - 1]) for d in range(1, WAYS)]
-    send_far(1)
+    relay_far(0)
+    relay_far(1)
     within(0, 3)
     arrive(waits)
     plane_sum[...] = sum(zs[i].astype(F32) for i in range(WAYS)).astype(BF16)
@@ -399,7 +381,6 @@
     for i in range(WAYS):
         total = total + zs[i].astype(F32) * jnp.where(i < z, 1.0, 0.0)
     within(3, 6)
-    relay_far(1)
     arrive(waits)
     ys[y] = plane_sum[...]
     for i in range(groups):
@@ -409,7 +390,6 @@
         total = total + xs[i].astype(F32)
     heads_in[x] = back[x]
     waits = [go(back.at[(x + d) % WAYS], heads_in.at[x], along_x[d - 1]) for d in range(1, WAYS)]
-    send_far(0)
     within(6, 8)
     arrive(waits)
     waits = [go(heads_in, sib2, sibling)]
@@ -428,13 +408,9 @@
                 denom[:, cols] + total[:, HEAD_DIM:]
             )
 
-    second_reduce(1)
     add_prior(base, heads_in)
-    relay_far(0)
     arrive(waits)
     add_prior((1 - c) * WAYS, sib2)
-    reduce_waits = gather_pieces(1)
-    second_reduce(0)
 
     @pl.loop(0, 2)
     def _(part):
@@ -446,7 +422,8 @@
         resid = resid.astype(BF16)
         resid_ref[part_rows, :] = resid
         ffn_ref[part_rows, :] = norm_rows(resid.astype(F32), fgain_ref[...]).astype(BF16)
-    arrive(reduce_waits + gather_pieces(0))
+    second_reduce(0)
+    second_reduce(1)
     for copy in copies:
         copy.wait_send()
 
@@ -464,7 +441,7 @@
     step = 2 * HEAD_DIM
     pieces = 3 * width // step
     count = 1 + 2 * (WAYS - 1) + groups - 1 + 2 + 3 * (WAYS - 1) + groups - 1
-    count += 3 + 12 + 4 * (WAYS - 1)
+    count += 3 + 12
 
     def wide(*shape):
         return pltpu.VMEM(shape + (packed,), BF16)
@@ -503,8 +480,6 @@
             wide(HALF),
             wide(2, WAYS - 1, SLICE),
             wide(2, 2, SLICE // 2),
-            wide(2, SLICE),
-            wide(2, WAYS - 1, PIECE),
             pltpu.SemaphoreType.DMA((pieces,)),
             pltpu.SemaphoreType.DMA((3,)),
             pltpu.SemaphoreType.DMA((count,)),
@@ -526,7 +501,7 @@
     gather, landed = rest[:chunks], rest[chunks : 2 * chunks]
     (
         hand, zs, relay, taken, made_rows, relay_back, hand_back, partial, final, local, send, recv,
-        base_ref, wg_ref, wu_ref, wd_ref, fetch_sem, inside, hotw, hot_inner, hot_out, hot_local, hot_send, hot_recv,
+        base_ref, wg_ref, wu_ref, wd_ref, fetch_sem, inside, pieces_in, whole, hotw, hot_inner, hot_out, hot_local, hot_send, hot_recv,
     ) = rest[2 * chunks :]
     depth = ROWS // chunks
     width = f_ref.shape[2]
@@ -549,7 +524,8 @@
         fetch = pltpu.make_async_copy(source, place_in, fetch_sem.at[n])
         fetch.start()
         fetched.append(fetch)
-    greet([sibling, mate, across, up, down])
+    far_x, far_z = at(z, x + 2, c), at(z + 2, x, c)
+    greet([sibling, mate, across, up, down, far_x, far_z])
     me = parity * CORES + c
     friend = (1 - parity) * CORES + c
     pending = []
@@ -702,7 +678,7 @@
         lax.fori_loop(0, blocks, run, 0)
 
     right, left = at(z, x + 1, c), at(z, x - 1, c)
-    ring = ((x, right, left), (z, up, down))
+    ring = ((x, right, left, far_x), (z, up, down, far_z))
     hot_made = {}
 
     def hot_go(n, src, dst, device):
@@ -717,10 +693,35 @@
         row = order * (HALF // 2) + ((spot + WAYS) % WAYS) * SLICE + shift
         return hotw.at[c, pl.ds(row, size)]
 
+    def hot_pieces():
+        for order in range(2):
+            spot, plus, minus, opposite = ring[1 - order]
+            for d, device in ((2, opposite), (1, plus), (3, minus)):
+                row = pl.ds(((spot + d) % WAYS) * PIECE, PIECE)
+                hot_go(
+                    32 + 6 * order + d, slice_ref.at[order, row], pieces_in.at[order, d - 1], device
+                )
+
+    def hot_sum():
+        for order in range(2):
+            spot, plus, minus, opposite = ring[1 - order]
+            for d in (1, 2, 3):
+                hot_made[32 + 6 * order + d].wait_recv()
+            row = pl.ds(pl.multiple_of(spot * PIECE, PIECE), PIECE)
+            total = slice_ref[order, row, :] + pieces_in[order, 0]
+            whole[order, row, :] = total + (pieces_in[order, 1] + pieces_in[order, 2])
+            for d, device in ((2, opposite), (1, plus), (3, minus)):
+                there = whole.at[order, row]
+                hot_go(35 + 6 * order + d, there, there, device)
+
+    def hot_whole(order):
+        for d in (1, 2, 3):
+            hot_made[35 + 6 * order + d].wait_recv()
+
     def hot_begin(order, part):
-        spot, plus, minus = ring[order]
+        spot, plus, minus, _ = ring[order]
         shift = part * short
-        piece = slice_ref.at[order, pl.ds(shift, short)]
+        piece = whole.at[order, pl.ds(shift, short)]
         there = hot_rows(order, spot, shift, short)
         base = 16 * order + 8 * part
         hot_go(base, piece, there, plus)
@@ -731,7 +732,7 @@
         hot_made["keep", order, part] = copy
 
     def hot_relay(order, part):
-        spot, plus, minus = ring[order]
+        spot, plus, minus, _ = ring[order]
         base = 16 * order + 8 * part
         shift = part * short
         for n, neighbour in ((0, spot - 1), (1, spot + 1)):
@@ -786,15 +787,17 @@
 
     stages = [widen, select, climb, forward, work, forward_back, give, mirror, build]
     begin(0)
+    hot_pieces()
     begin(1)
-    hot_begin(1, 0)
-    hot_begin(1, 1)
     extras = {
-        2: ((hot_relay, 1, 0), (hot_begin, 0, 0)),
-        3: ((hot_relay, 1, 1),),
-        4: ((hot_last, 1, 0), (hot_relay, 0, 0)),
-        5: ((hot_last, 1, 1), (hot_begin, 0, 1)),
-        7: ((hot_last, 0, 0), (hot_relay, 0, 1)),
+        0: ((hot_sum,),),
+        1: ((hot_whole, 1), (hot_begin, 1, 0), (hot_begin, 1, 1)),
+        2: ((hot_whole, 0), (hot_begin, 0, 0)),
+        3: ((hot_relay, 1, 0),),
+        4: ((hot_relay, 1, 1), (hot_relay, 0, 0)),
+        5: ((hot_last, 1, 0), (hot_begin, 0, 1)),
+        6: ((hot_last, 1, 1), (hot_last, 0, 0)),
+        7: ((hot_relay, 0, 1),),
         9: ((hot_last, 0, 1),),
         chunks + 3: ((hot_ready,), (hot_first,)),
         chunks + 4: ((hot_second,),),
@@ -851,12 +854,14 @@
             pltpu.VMEM(w_down.shape, BF16),
             pltpu.SemaphoreType.DMA((4,)),
             pltpu.VMEM((WAYS * PART * depth, w_gate.shape[1]), BF16),
+            pltpu.VMEM((2, WAYS - 1, PIECE, packed), BF16),
+            pltpu.VMEM((2, SLICE, packed), BF16),
             pltpu.VMEM((CORES, HALF, packed), BF16),
             pltpu.VMEM((2 * rows, w_gate.shape[1]), BF16),
             pltpu.VMEM((2, rows, width), BF16),
             pltpu.SemaphoreType.DMA((4,)),
-            pltpu.SemaphoreType.DMA((32,)),
-            pltpu.SemaphoreType.DMA((32,)),
+            pltpu.SemaphoreType.DMA((48,)),
+            pltpu.SemaphoreType.DMA((48,)),
         ],
         compiler_params=pltpu.CompilerParams(
             collective_id=1, has_side_effects=True, vmem_limit_bytes=67043328

time: 221 us -> 222 us (level)
    pallas_call x1, Pallas kernels: 144 us -> 157 us  [moe(): pl.pallas_call(functools.partial(moe_kernel, blocks, chunks), out_shape=j...]
    pallas_call x1, Pallas kernels: 68.4 us -> 56.9 us  [front(): pl.pallas_call(functools.partial(front_kernel, groups, blocks), out_shape...]
where the time goes in v3:
time: 222 us; the launch traced here: 219 us
  Pallas kernels  214 us (96%)
  local copies, waits for them, and re-layouts  4.04 us (2%)
    pallas_call x1, Pallas kernels, moe(): pl.pallas_call(functools.partial(moe_kernel, blocks, chunks), out_shape=j...  157 us
    pallas_call x1, Pallas kernels, front(): pl.pallas_call(functools.partial(front_kernel, groups, blocks), out_shape...  56.9 us

profile of v3, /device:TPU:24, one launch (start us, length us, event | category | flops | bytes accessed | tf_op | source)
XLA Modules:
  0.0 218.8 jit_solution(13279329351737014810)
XLA Ops:
  0.0 56.9 %front.1 = (bf16[896,1024]{1,0:T(8,128)(2,1)}, bf16[896,1024]{1,0:T(8,128)(2,1)}, s32[24,128]{1,0:T(8,128)S(1)}, f32[8,128]{1,0:T(8,128)}, bf16[2,64,2816]{2,1,0:T(8,128)(2,1)}) custom-call(s32[2,7]{1,0:T(2,128)} %bitcast.33, s32[2,7]{1,0:T(2,128)} %bitcast.34, bf16[896,1024]{1,0:T(8,128)(2,1)} %x_ref.1, f32[1,1024]{1,0:T(1,128)} %bitcast.30, ...), custom_call_target="tpu_custom_call" | custom-call | tf_op jit(solution)/shard_map/front/pallas_call | solution.py:451
  56.9 0.0 copy-start
  56.9 0.6 copy-done
  57.5 0.6 slice.3
  58.7 157.1 %moe.6 = bf16[7,128,1024]{2,1,0:T(8,128)(2,1)} custom-call(s32[24,128]{1,0:T(8,128)} %copy-done, f32[8,128]{1,0:T(8,128)} %get-tuple-element.295.weight, bf16[7,128,1024]{2,1,0:T(8,128)(2,1)} %bitcast.27, bf16[7,128,1024]{2,1,0:T(8,128)(2,1)} %bitcast.29, bf16[1024,896]{1,0:T(8,128)(2,1)} %bitcast.19, bf16[1024,896]{1,0:T(8,128)(2,1)} %bitcast.22, ...), custom_call_target="tpu_custom_call" | custom-call | tf_op jit(solution)/shard_map/moe/pallas_call | solution.py:831
  215.9 2.9 %copy.26 = bf16[896,1024]{1,0:T(8,128)(2,1)} copy(bf16[896,1024]{1,0:T(8,128)(2,1)} %get-tuple-element.184) | data formatting | bytes 3670016
  (1 shorter events, 0.0 us)
Async XLA Ops:
  56.9 0.6 copy-start

commit v4 on v1

--- a/solution.py
+++ b/solution.py
@@ -16,7 +16,7 @@
 SLOTS = 2
 SIDES = 2
 PART = SIDES * SLOTS
-CHUNKS = 8
+DEPTHS = (8, 16, 16, 16, 16, 16, 16, 16, 8)
 STATE = 144
 LIMIT = 8
 LANES = 128
@@ -519,12 +519,11 @@
     blocks, chunks, table, weight, f_ref, base_ref, wg_ref, wu_ref, wd_ref, slice_ref, out_ref,
     *rest
 ):
-    gather, landed = rest[:chunks], rest[chunks : 2 * chunks]
-    (
-        hand, zs, relay, taken, made_rows, relay_back, hand_back, partial, final, local, send, recv,
-        inside, hotw, hot_inner, hot_out, hot_local, hot_send, hot_recv,
-    ) = rest[2 * chunks :]
-    depth = ROWS // chunks
+    lists = [rest[n * chunks : (n + 1) * chunks] for n in range(11)]
+    gather, landed, hand, zs, relay, taken, made_rows, relay_back, hand_back, partial, final = lists
+    local, send, recv, inside, hotw, hot_inner, hot_out, hot_local, hot_send, hot_recv = rest[
+        11 * chunks :
+    ]
     width = f_ref.shape[2]
     hidden = wg_ref.shape[1]
     y, z, x, c = place()
@@ -563,7 +562,7 @@
         return (row + WAYS) % WAYS
 
     def begin(k):
-        own = f_ref.at[:, pl.ds(k * depth, depth), :]
+        own = f_ref.at[:, pl.ds(sum(DEPTHS[:k]), DEPTHS[k]), :]
         here = gather[k].at[pl.ds(me * blocks, blocks)]
         go(k, 0, own, here, mate)
         go(k, 1, own, here, sibling)
@@ -579,34 +578,34 @@
         arrived(k, 1, 2)
         for row in range(WAYS):
             for j in range(SLOTS):
-                hand[k, row, j] = gather[k][table[8 + row * SLOTS + j, 0]]
-        go(k, 3, hand.at[k], zs.at[k, :, 1], across)
+                hand[k][row, j] = gather[k][table[8 + row * SLOTS + j, 0]]
+        go(k, 3, hand[k], zs[k].at[:, 1], across)
         for row in range(WAYS):
             for j in range(SLOTS):
-                zs[k, row, 0, j] = gather[k][table[row * SLOTS + j, 0]]
+                zs[k][row, 0, j] = gather[k][table[row * SLOTS + j, 0]]
 
     def climb(k):
         arrived(k, 3)
-        go(k, 6, zs.at[k, step_of(z + 2), 0], relay.at[k, 0], up)
-        go(k, 19, zs.at[k, step_of(z + 2), 1], relay.at[k, 1], down)
-        go(k, 4, zs.at[k, step_of(z + 1)], taken.at[k, z], up)
-        go(k, 5, zs.at[k, step_of(z - 1)], taken.at[k, z], down)
-        keep(k, 1, zs.at[k, z], taken.at[k, z])
+        go(k, 6, zs[k].at[step_of(z + 2), 0], relay[k].at[0], up)
+        go(k, 19, zs[k].at[step_of(z + 2), 1], relay[k].at[1], down)
+        go(k, 4, zs[k].at[step_of(z + 1)], taken[k].at[z], up)
+        go(k, 5, zs[k].at[step_of(z - 1)], taken[k].at[z], down)
+        keep(k, 1, zs[k].at[z], taken[k].at[z])
 
     def forward(k):
         arrived(k, 6)
-        go(k, 7, relay.at[k, 0], taken.at[k, step_of(z - 1), 0], up)
+        go(k, 7, relay[k].at[0], taken[k].at[step_of(z - 1), 0], up)
         arrived(k, 19)
-        go(k, 20, relay.at[k, 1], taken.at[k, step_of(z + 1), 1], down)
+        go(k, 20, relay[k].at[1], taken[k].at[step_of(z + 1), 1], down)
 
     def work(k):
         arrived(k, 4, 5, 7, 20)
         made[k, "keep", 1].wait()
         def rise(cols):
-            rows = taken[k].reshape(WAYS * PART * depth, width)
+            rows = taken[k][...].reshape(WAYS * PART * DEPTHS[k], width)
             gate = jnp.dot(rows, wg_ref[:, cols], preferred_element_type=F32)
             upper = jnp.dot(rows, wu_ref[:, cols], preferred_element_type=F32)
-            inside[:, cols] = (jax.nn.silu(gate) * upper).astype(BF16)
+            inside[: rows.shape[0], cols] = (jax.nn.silu(gate) * upper).astype(BF16)
 
         @pl.loop(0, hidden // TILE)
         def _(i):
@@ -618,32 +617,32 @@
         @pl.loop(0, width // TILE)
         def _(i):
             cols = pl.ds(pl.multiple_of(i * TILE, TILE), TILE)
-            result = jnp.dot(inside[...], wd_ref[:, cols], preferred_element_type=F32)
-            made_rows[k, :, :, :, :, cols] = result.astype(BF16).reshape(
-                WAYS, SIDES, SLOTS, depth, TILE
+            result = jnp.dot(inside[: WAYS * PART * DEPTHS[k], :], wd_ref[:, cols], preferred_element_type=F32)
+            made_rows[k][:, :, :, :, cols] = result.astype(BF16).reshape(
+                WAYS, SIDES, SLOTS, DEPTHS[k], TILE
             )
 
-        go(k, 12, made_rows.at[k, step_of(z + 2), 0], relay_back.at[k, 0], up)
-        go(k, 21, made_rows.at[k, step_of(z + 2), 1], relay_back.at[k, 1], down)
+        go(k, 12, made_rows[k].at[step_of(z + 2), 0], relay_back[k].at[0], up)
+        go(k, 21, made_rows[k].at[step_of(z + 2), 1], relay_back[k].at[1], down)
         for n, d, device in ((8, 1, up), (10, -1, down)):
             target = step_of(z + d)
-            go(k, n, made_rows.at[k, target, 0], landed[k].at[pl.ds(c * 16 + z * SLOTS, SLOTS)], device)
-            go(k, n + 1, made_rows.at[k, target, 1], hand_back.at[k, pl.ds(z * SLOTS, SLOTS)], device)
-        keep(k, 2, made_rows.at[k, z, 0], landed[k].at[pl.ds(c * 16 + z * SLOTS, SLOTS)])
-        keep(k, 3, made_rows.at[k, z, 1], hand_back.at[k, pl.ds(z * SLOTS, SLOTS)])
+            go(k, n, made_rows[k].at[target, 0], landed[k].at[pl.ds(c * 16 + z * SLOTS, SLOTS)], device)
+            go(k, n + 1, made_rows[k].at[target, 1], hand_back[k].at[pl.ds(z * SLOTS, SLOTS)], device)
+        keep(k, 2, made_rows[k].at[z, 0], landed[k].at[pl.ds(c * 16 + z * SLOTS, SLOTS)])
+        keep(k, 3, made_rows[k].at[z, 1], hand_back[k].at[pl.ds(z * SLOTS, SLOTS)])
 
     def forward_back(k):
         arrived(k, 21)
         origin = step_of(z + 1)
-        go(k, 14, relay_back.at[k, 1], hand_back.at[k, pl.ds(origin * SLOTS, SLOTS)], down)
+        go(k, 14, relay_back[k].at[1], hand_back[k].at[pl.ds(origin * SLOTS, SLOTS)], down)
         arrived(k, 12)
         origin = step_of(z - 1)
-        go(k, 13, relay_back.at[k, 0], landed[k].at[pl.ds(c * 16 + origin * SLOTS, SLOTS)], up)
+        go(k, 13, relay_back[k].at[0], landed[k].at[pl.ds(c * 16 + origin * SLOTS, SLOTS)], up)
 
     def give(k):
         arrived(k, 9, 11, 14)
         made[k, "keep", 3].wait()
-        go(k, 15, hand_back.at[k], landed[k].at[pl.ds(c * 16 + 8, 8)], across)
+        go(k, 15, hand_back[k], landed[k].at[pl.ds(c * 16 + 8, 8)], across)
         arrived(k, 8, 10, 13)
         made[k, "keep", 2].wait()
         there = landed[k].at[pl.ds(c * 16, 8)]
@@ -662,23 +661,23 @@
                 first = start + 2 * b
                 total = landed[k][table[16, first]].astype(F32) * weight[0, first]
                 total = total + landed[k][table[16, first + 1]].astype(F32) * weight[0, first + 1]
-                partial[k, offset + b] = total.astype(BF16)
+                partial[k][offset + b] = total.astype(BF16)
                 return carry
 
             return run
 
         row = (x // 2) * 4 * 2 * blocks
         lax.fori_loop(0, blocks, one(row + friend * 2 * blocks, blocks), 0)
-        go(k, 18, partial.at[k, pl.ds(blocks, blocks)], final.at[k], mate)
+        go(k, 18, partial[k].at[pl.ds(blocks, blocks)], final[k], mate)
         lax.fori_loop(0, blocks, one(row + me * 2 * blocks, 0), 0)
 
     def finish(k):
         arrived(k, 18)
-        rows = slice(k * depth, (k + 1) * depth)
+        rows = slice(sum(DEPTHS[:k]), sum(DEPTHS[: k + 1]))
 
         def run(b, carry):
-            total = base_ref[b, rows, :].astype(F32) + partial[k, b].astype(F32)
-            total = total + final[k, b].astype(F32)
+            total = base_ref[b, rows, :].astype(F32) + partial[k][b].astype(F32)
+            total = total + final[k][b].astype(F32)
             for i in range(2):
                 share = jnp.where(table[21, i] == b, weight[2, i], 0.0)
                 total = total + hot_out[i, rows, :].astype(F32) * share
@@ -806,8 +805,12 @@
 def moe(table, weight, ffn_in, base, w_gate, w_up, w_down, hot_slices):
     blocks, rows, width = ffn_in.shape
     packed = hot_slices.shape[2]
-    chunks = CHUNKS
-    depth = rows // chunks
+    chunks = len(DEPTHS)
+    depth = max(DEPTHS)
+
+    def each(*shape):
+        return [pltpu.VMEM(shape + (deep, width), BF16) for deep in DEPTHS]
+
     pair = 2 * CORES * blocks
     whole = pl.BlockSpec(memory_space=pltpu.VMEM)
     return pl.pallas_call(
@@ -815,18 +818,18 @@
         out_shape=jax.ShapeDtypeStruct(base.shape, BF16),
         in_specs=[pl.BlockSpec(memory_space=pltpu.SMEM)] * 2 + [whole] * 6,
         out_specs=whole,
-        scratch_shapes=[pltpu.VMEM((pair, depth, width), BF16)] * chunks
-        + [pltpu.VMEM((CORES * 16, depth, width), BF16)] * chunks
+        scratch_shapes=each(pair)
+        + each(CORES * 16)
+        + each(WAYS, SLOTS)
+        + each(WAYS, SIDES, SLOTS)
+        + each(SIDES, SLOTS)
+        + each(WAYS, SIDES, SLOTS)
+        + each(WAYS, SIDES, SLOTS)
+        + each(SIDES, SLOTS)
+        + each(WAYS * SLOTS)
+        + each(2 * blocks)
+        + each(blocks)
         + [
-            pltpu.VMEM((chunks, WAYS, SLOTS, depth, width), BF16),
-            pltpu.VMEM((chunks, WAYS, SIDES, SLOTS, depth, width), BF16),
-            pltpu.VMEM((chunks, SIDES, SLOTS, depth, width), BF16),
-            pltpu.VMEM((chunks, WAYS, SIDES, SLOTS, depth, width), BF16),
-            pltpu.VMEM((chunks, WAYS, SIDES, SLOTS, depth, width), BF16),
-            pltpu.VMEM((chunks, SIDES, SLOTS, depth, width), BF16),
-            pltpu.VMEM((chunks, WAYS * SLOTS, depth, width), BF16),
-            pltpu.VMEM((chunks, 2 * blocks, depth, width), BF16),
-            pltpu.VMEM((chunks, blocks, depth, width), BF16),
             pltpu.SemaphoreType.DMA((chunks, 4)),
             pltpu.SemaphoreType.DMA((chunks, 22)),
             pltpu.SemaphoreType.DMA((chunks, 22)),

time: 213 us -> 213 us (level)
  no operation moved by 1% of the time
where the time goes in v4:
time: 213 us; the launch traced here: 210 us
  Pallas kernels  206 us (97%)
  local copies, waits for them, and re-layouts  4.04 us (2%)
    pallas_call x1, Pallas kernels, moe(): pl.pallas_call(functools.partial(moe_kernel, blocks, chunks), out_shape=j...  147 us
    pallas_call x1, Pallas kernels, front(): pl.pallas_call(functools.partial(front_kernel, groups, blocks), out_shape...  58.8 us

profile of v4, /device:TPU:24, one launch (start us, length us, event | category | flops | bytes accessed | tf_op | source)
XLA Modules:
  0.0 210.2 jit_solution(6745089253245338076)
XLA Ops:
  0.0 58.8 %front.1 = (bf16[896,1024]{1,0:T(8,128)(2,1)}, bf16[896,1024]{1,0:T(8,128)(2,1)}, s32[24,128]{1,0:T(8,128)S(1)}, f32[8,128]{1,0:T(8,128)}, bf16[2,64,2816]{2,1,0:T(8,128)(2,1)}) custom-call(s32[2,7]{1,0:T(2,128)} %bitcast.33, s32[2,7]{1,0:T(2,128)} %bitcast.34, bf16[896,1024]{1,0:T(8,128)(2,1)} %x_ref.1, f32[1,1024]{1,0:T(1,128)} %bitcast.30, ...), custom_call_target="tpu_custom_call" | custom-call | tf_op jit(solution)/shard_map/front/pallas_call | solution.py:470
  58.8 0.0 copy-start
  58.8 0.6 copy-done
  59.4 0.6 slice.3
  60.6 146.7 %moe.6 = bf16[7,128,1024]{2,1,0:T(8,128)(2,1)} custom-call(s32[24,128]{1,0:T(8,128)} %copy-done, f32[8,128]{1,0:T(8,128)} %get-tuple-element.295.weight, bf16[7,128,1024]{2,1,0:T(8,128)(2,1)} %bitcast.27, bf16[7,128,1024]{2,1,0:T(8,128)(2,1)} %bitcast.29, bf16[1024,896]{1,0:T(8,128)(2,1)} %bitcast.19, bf16[1024,896]{1,0:T(8,128)(2,1)} %bitcast.22, ...), custom_call_target="tpu_custom_call" | custom-call | tf_op jit(solution)/shard_map/moe/pallas_call | solution.py:816
  207.4 2.9 %copy.26 = bf16[896,1024]{1,0:T(8,128)(2,1)} copy(bf16[896,1024]{1,0:T(8,128)(2,1)} %get-tuple-element.184) | data formatting | bytes 3670016
  (1 shorter events, 0.0 us)
Async XLA Ops:
  58.8 0.6 copy-start
